TPU v7x, 512 devices: a whole 4x8x8 slice. The times are simulated.
512 devices in a mesh: grp: 2 (over core), mer: 64 (over y, z), sub: 4 (over x).
Axes of the slice: x: 4, y: 8, z: 8, core: 2. Of those that a mesh axis runs over, the one named last changes fastest.
Arguments:
- field: float32 [2, 256, 262144], P('grp', 'sub', 'mer'), may hold values from -6 to 6
- previous: float32 [2, 256, 262144], P('grp', 'sub', 'mer'), may hold values from -6 to 6
- stiff: float32 [2, 128, 128], P('grp'), as said below
- synth: float32 [2, 256, 256], P('grp', None, 'sub'), may hold values from -0.5 to 0.5
- owner: int32 [2, 16384, 1], P('grp', 'mer'), may hold values from 0 to 63; in each aligned block of 256 rows (0 to 255, 256 to 511, ..., all dimensions but the last counted through in order) at most 8 rows name the same one
- face: int32 [2, 16384], P('grp', 'mer'), may hold values from 0 to 255
- weight: float32 [2, 16384], P('grp', 'mer'), may hold values from 0.3 to 1.7
Outputs:
- latest: float32 [2, 256, 262144], P('grp', 'sub', 'mer')
- prior: float32 [2, 256, 262144], P('grp', 'sub', 'mer')
Inputs may be any that keep to these rules, and one draw needn't show every extreme that they name: Among the 256 interface points of one domain, at most 8 name the same owner, and in some domains exactly 8 do. `stiff`: each model's element matrix is symmetric.
All inputs are finite; a program needn't handle non-finite values.
Results may differ from a plain program's by a relative error of at most 0.0001.
Values sent between devices are 32-bit elements; how exact they have to be, the bound alone decides.
A program may use at most 64 MiB of HBM per device.

v0:
```python
import jax
import jax.numpy as jnp
from jax import lax
from jax.sharding import PartitionSpec as P

ITERS = 2


DT2 = 0.5
KAPPA = 0.5


def extended(value, sides, width):
    for axis, dim in sides:
        peers, length = (lax.axis_size(axis), value.shape[dim])
        up = [(i, (i + 1) % peers) for i in range(peers - 1)]
        down = [(j, i) for i, j in up]
        last = lax.slice_in_dim(value, length - width, length, axis=dim)
        initial = lax.slice_in_dim(value, 0, width, axis=dim)
        before = lax.ppermute(last, axis, up)
        after = lax.ppermute(initial, axis, down)
        value = jnp.concatenate([before, value, after], axis=dim)
    return value


def split_up(value, dim, peers):
    lengths = value.shape
    blocks = value.reshape(*lengths[:dim], peers, lengths[dim] // peers, *lengths[dim + 1 :])
    return jnp.moveaxis(blocks, dim, 0)


def sum_at_owner(value, axis, dim):
    blocks = split_up(value, dim, lax.axis_size(axis))
    arrived = lax.all_to_all(blocks, axis, split_axis=0, concat_axis=0, tiled=True)
    return arrived.sum(axis=0)


def sent_together(arrays, axis, split_dim, concat_dim, along):
    columns = [a.reshape(*a.shape[:along], -1) for a in arrays]
    both = jnp.concatenate(columns, axis=along)
    out, at, gathered = (
        lax.all_to_all(both, axis, split_axis=split_dim, concat_axis=concat_dim, tiled=True),
        0,
        [],
    )
    for a, column in zip(arrays, columns):
        slab = out[..., at : at + column.shape[along]]
        gathered.append(slab.reshape(*slab.shape[:along], *a.shape[along:]))
        at += column.shape[along]
    return tuple(gathered)


def swapped(value, axis, stride):
    return lax.ppermute(value, axis, [(i, i ^ 1 << stride) for i in range(lax.axis_size(axis))])


def body(field, previous, stiff, synth, owner, face, weight):
    state = field[0]
    older = previous[0]
    matrix = stiff[0]
    table = synth[0]
    owners = owner[0, :, 0]
    faces = face[0]
    weights = weight[0]
    rows = state.shape[0]
    points = state.shape[1]
    iface = owners.shape[0]
    elems = matrix.shape[0]
    domains = lax.axis_size("mer")
    width = 2 * iface // domains
    member = (owners[:, None] == jnp.arange(domains, dtype=jnp.int32)[None, :]).astype(jnp.int32)
    ranks = jnp.sum((jnp.cumsum(member, axis=0) - 1) * member, axis=1)
    slot_labels = (
        jnp.full((domains, width), float(iface), jnp.float32)
        .at[owners, ranks]
        .set(faces.astype(jnp.float32))
    )
    for step in range(ITERS):
        padded = extended(state, (("mer", 1),), 1)
        lap = 2.0 * state - padded[:, 2:] - padded[:, :-2]
        blocks = state.reshape(rows, points // elems, elems)
        stiffened = jnp.einsum(
            "cne,ef->cnf", blocks, matrix, precision=lax.Precision.HIGHEST
        ).reshape(rows, points)
        surface = state[:, :iface]
        traces = (
            sum_at_owner(
                jnp.dot(
                    table,
                    surface,
                    precision=lax.Precision.HIGHEST,
                    preferred_element_type=jnp.float32,
                ),
                "sub",
                0,
            )
            * weights[None, :]
        )
        packed = jnp.zeros((domains, width, rows), jnp.float32).at[owners, ranks].set(traces.T)
        got, got_labels = sent_together((packed, slot_labels), "mer", 0, 0, 2)
        target = got_labels.reshape(-1).astype(jnp.int32)
        summed = jax.ops.segment_sum(got.reshape(-1, rows), target, num_segments=iface + 1)
        crossed = swapped(summed[:iface].T, "grp", 0)
        forcing = jnp.pad(crossed, ((0, 0), (0, points - iface)))
        newer = 2.0 * state - older + DT2 * (forcing - stiffened - KAPPA * lap)
        state, older = (newer, state)
    return (state[None, :, :], older[None, :, :])


def solution(mesh):
    in_specs = (
        P("grp", "sub", "mer"),
        P("grp", "sub", "mer"),
        P("grp", None, None),
        P("grp", None, "sub"),
        P("grp", "mer", None),
        P("grp", "mer"),
        P("grp", "mer"),
    )
    out_specs = (P("grp", "sub", "mer"), P("grp", "sub", "mer"))
    return jax.shard_map(body, mesh=mesh, in_specs=in_specs, out_specs=out_specs, check_vma=False)
```

profile of v0, /device:TPU:1, one launch (start us, length us, event | category | flops | bytes accessed | tf_op | source)
XLA Modules:
  0.0 132.3 jit_solution(9078206508141066388)
XLA Ops:
  1.6 1.9 %fusion.23 = f32[4,64,256]{2,1,0:T(8,128)} fusion(f32[4,64,64]{2,1,0:T(8,128)S(1)} %bitcast.107, f32[64,4096]{1,0:T(8,128)} %bitcast.96), kind=kOutput, calls=%fused_computation.43 | convolution fusion | flops 50331648 | bytes 393216 | tf_op jit(solution)/shard_map/dot_general | solution.py:88
  3.5 5.0 %all-to-all-start = ((f32[4,64,256]{2,1,0:T(8,128)}), f32[4,64,256]{2,1,0:T(8,128)S(1)}, u32[]{:S(2)}, u32[]{:S(2)}) async-start(f32[4,64,256]{2,1,0:T(8,128)} %fusion.23), calls=%async_computation | async-start | bytes 524288 | tf_op jit(solution)/shard_map/all_to_all | solution.py:34
  10.2 11.3 %scatter_fusion.1 = f32[64,8]{0,1:T(8,128)S(1)} fusion(f32[64,8]{0,1:T(8,128)S(1)} %broadcast_in_dim.6, s32[256]{0:T(256)S(1)} %bitcast.93, f32[256]{0:T(256)S(1)} %bitcast.115), kind=kCustom, calls=%fused_computation.1 | custom fusion | bytes 5120 | tf_op jit(solution)/shard_map/scatter | solution.py:76
  22.5 11.5 %scatter_fusion = f32[64,8,64]{2,1,0:T(8,128)S(1)} fusion(f32[64,8,64]{2,1,0:T(8,128)S(1)} %broadcast.80.clone, s32[256]{0:T(256)S(1)} %bitcast.94, f32[256,64]{1,0:T(8,128)S(1)} %copy.21), kind=kCustom, calls=%fused_computation | custom fusion | bytes 198656 | tf_op jit(solution)/shard_map/scatter | solution.py:99
  34.9 16.3 %all-to-all-start.1 = ((f32[64,8,65]{2,1,0:T(8,128)}), f32[64,8,65]{2,1,0:T(8,128)S(1)}, u32[]{:S(2)}, u32[]{:S(2)}) async-start(f32[64,8,65]{2,1,0:T(8,128)} %pad_maximum_fusion.4), calls=%async_computation.1 | async-start | bytes 524288 | tf_op jit(solution)/shard_map/all_to_all | solution.py:42
  51.3 1.3 collective-permute-start.1
  52.6 4.0 %collective-permute-start.2 = (f32[64,1]{1,0:T(8,128)S(1)}, f32[64,1]{1,0:T(8,128)S(1)}, u32[]{:S(2)}, u32[]{:S(2)}) collective-permute-start(f32[64,1]{1,0:T(8,128)S(1)} %get-tuple-element.5), channel_id=1, source_target_pairs={{0,4},{4,8},{8,12},{12,16},{16,20},{20,24},{24,28},{28,32},{32,36}... | collective-permute-start | bytes 776 | tf_op jit(solution)/shard_map/ppermute | solution.py:20
  56.8 6.9 %all-to-all-done.1 = f32[64,8,65]{2,1,0:T(8,128)S(1)} async-done(((f32[64,8,65]{2,1,0:T(8,128)}), f32[64,8,65]{2,1,0:T(8,128)S(1)}, u32[]{:S(2)}, u32[]{:S(2)}) %all-to-all-start.1) | async-done | bytes 133152 | tf_op jit(solution)/shard_map/all_to_all | solution.py:42
  63.7 1.2 fusion.16
  65.0 3.2 %scatter_custom_fusion.2 = f32[257,64]{1,0:T(8,128)S(1)} fusion(s32[512]{0:T(512)S(1)} %reshape.134, f32[64,8,65]{2,1,0:T(8,128)S(1)} %all-to-all-done.1, f32[]{:T(128)} %constant.9.clone.1), kind=kCustom, calls=%fused_computation.30 | custom fusion | flops 32768 | bytes 327940 | tf_op jit(solution)/shard_map/scatter-add | solution.py:102
  68.3 5.4 %collective-permute-start = (f32[64,256]{1,0:T(8,128)S(1)}, f32[64,256]{1,0:T(8,128)S(1)}, u32[]{:S(2)}, u32[]{:S(2)}) collective-permute-start(f32[64,256]{1,0:T(8,128)S(1)} %bitcast.108), channel_id=1, source_target_pairs={{0,256},{256,0},{1,257},{257,1},{2,258},{258,2},{3,259},{259,3},{4... | collective-permute-start | bytes 196616 | tf_op jit(solution)/shard_map/ppermute | solution.py:54
  73.7 1.0 fusion.27
  74.9 1.2 fusion.6
  76.6 10.6 %all_to_all.20 = f32[4,64,256]{2,1,0:T(8,128)S(1)} all-to-all(f32[4,64,256]{2,1,0:T(8,128)S(1)} %bitcast.106), channel_id=1, replica_groups=mesh['grp'=2,'mer'=64,'sub'=4] {'sub'}, dimensions={0} | all-to-all | bytes 524288 | tf_op jit(solution)/shard_map/all_to_all | solution.py:34
  87.3 11.5 %scatter_fusion.2 = f32[64,8,64]{2,1,0:T(8,128)S(1)} fusion(f32[64,8,64]{2,1,0:T(8,128)S(1)} %broadcast.80, s32[256]{0:T(256)S(1)} %bitcast.95, f32[256,64]{1,0:T(8,128)S(1)} %copy.24), kind=kCustom, calls=%fused_computation.3 | custom fusion | bytes 198656 | tf_op jit(solution)/shard_map/scatter | solution.py:99
  99.7 4.6 %all-to-all-start.3 = ((f32[64,8,65]{2,1,0:T(8,128)}), f32[64,8,65]{2,1,0:T(8,128)S(1)}, u32[]{:S(2)}, u32[]{:S(2)}) async-start(f32[64,8,65]{2,1,0:T(8,128)} %pad_maximum_fusion.5), calls=%async_computation.3 | async-start | bytes 524288 | tf_op jit(solution)/shard_map/all_to_all | solution.py:42
  105.0 1.3 collective-permute-start.4
  106.3 4.6 %collective-permute-start.5 = (f32[64,1]{1,0:T(8,128)}, f32[64,1]{1,0:T(8,128)}, u32[]{:S(2)}, u32[]{:S(2)}) collective-permute-start(f32[64,1]{1,0:T(8,128)} %get-tuple-element.3), channel_id=1, source_target_pairs={{0,4},{4,8},{8,12},{12,16},{16,20},{20,24},{24,28},{28,32},{32,36}... | collective-permute-start | bytes 776 | tf_op jit(solution)/shard_map/ppermute | solution.py:20
  111.1 5.7 %all-to-all-done.3 = f32[64,8,65]{2,1,0:T(8,128)S(1)} async-done(((f32[64,8,65]{2,1,0:T(8,128)}), f32[64,8,65]{2,1,0:T(8,128)S(1)}, u32[]{:S(2)}, u32[]{:S(2)}) %all-to-all-start.3) | async-done | bytes 133152 | tf_op jit(solution)/shard_map/all_to_all | solution.py:42
  116.8 1.2 fusion.14
  118.1 3.8 %scatter_custom_fusion.4 = f32[257,64]{1,0:T(8,128)} fusion(s32[512]{0:T(512)S(1)} %reshape.148, f32[64,8,65]{2,1,0:T(8,128)S(1)} %all-to-all-done.3, f32[]{:T(128)} %constant.9.clone.1), kind=kCustom, calls=%fused_computation.26 | custom fusion | flops 32768 | bytes 327940 | tf_op jit(solution)/shard_map/scatter-add | solution.py:102
  123.0 5.5 %collective-permute-start.3 = (f32[64,256]{1,0:T(8,128)S(1)}, f32[64,256]{1,0:T(8,128)S(1)}, u32[]{:S(2)}, u32[]{:S(2)}) collective-permute-start(f32[64,256]{1,0:T(8,128)S(1)} %bitcast.109), channel_id=1, source_target_pairs={{0,256},{256,0},{1,257},{257,1},{2,258},{258,2},{3,259},{259,3},{4... | collective-permute-start | bytes 196616 | tf_op jit(solution)/shard_map/ppermute | solution.py:54
  128.4 1.0 fusion.25
  129.5 2.9 %fusion.3 = f32[1,64,4096]{2,1,0:T(8,128)} fusion(f32[8,8,32,128]{3,2,1,0:T(8,128)S(1)} %bitcast.105, f32[64,4096]{1,0:T(8,128)S(1)} %fusion.6, f32[64,1]{1,0:T(8,128)} %collective-permute-done.5, f32[64,1]{1,0:T(8,128)S(1)} %collective-permute-done.4, f32[64,256]{1,0:T(8,128)S(1)} %collective-permute-done.3, f32[1,64,4096]{2,1,0:T(8,128)S(1)} %copy-done.1), kind=kLoop, calls=%fused_computation.9 | loop fusion | flops 2883584 | bytes 4260352 | tf_op jit(solution)/shard_map/broadcast_in_dim | solution.py:107
  (56 shorter events, 8.5 us)
Async XLA Ops:
  0.6 73.1 %copy-start = (f32[1,128,128]{2,1,0:T(8,128)S(1)}, f32[1,128,128]{2,1,0:T(8,128)}, u32[]{:S(2)}) copy-start(f32[1,128,128]{2,1,0:T(8,128)} %param.9) | copy-start | bytes 196612
  3.5 5.0 %copy-start.7 = (s32[1,256]{1,0:T(1,128)S(1)}, s32[1,256]{1,0:T(1,128)}, u32[]{:S(2)}) copy-start(s32[1,256]{1,0:T(1,128)} %param.12) | copy-start | bytes 3076
  3.5 18.2 %all-to-all-start = ((f32[4,64,256]{2,1,0:T(8,128)}), f32[4,64,256]{2,1,0:T(8,128)S(1)}, u32[]{:S(2)}, u32[]{:S(2)}) async-start(f32[4,64,256]{2,1,0:T(8,128)} %fusion.23), calls=%async_computation | async-start | bytes 524288 | tf_op jit(solution)/shard_map/all_to_all | solution.py:34
  8.5 0.7 copy-start.5
  21.7 0.7 copy-start.6
  22.5 28.7 %copy-start.1 = (f32[1,64,4096]{2,1,0:T(8,128)S(1)}, f32[1,64,4096]{2,1,0:T(8,128)}, u32[]{:S(2)}) copy-start(f32[1,64,4096]{2,1,0:T(8,128)} %param.7) | copy-start | bytes 3145732
  34.9 28.8 %all-to-all-start.1 = ((f32[64,8,65]{2,1,0:T(8,128)}), f32[64,8,65]{2,1,0:T(8,128)S(1)}, u32[]{:S(2)}, u32[]{:S(2)}) async-start(f32[64,8,65]{2,1,0:T(8,128)} %pad_maximum_fusion.4), calls=%async_computation.1 | async-start | bytes 524288 | tf_op jit(solution)/shard_map/all_to_all | solution.py:42
  51.3 23.4 %collective-permute-start.1 = (f32[64,1]{1,0:T(8,128)S(1)}, f32[64,1]{1,0:T(8,128)S(1)}, u32[]{:S(2)}, u32[]{:S(2)}) collective-permute-start(f32[64,1]{1,0:T(8,128)S(1)} %get-tuple-element.4), channel_id=1, source_target_pairs={{4,0},{8,4},{12,8},{16,12},{20,16},{24,20},{28,24},{32,28},{36,32}... | collective-permute-start | bytes 776 | tf_op jit(solution)/shard_map/ppermute | solution.py:21
  52.6 22.1 %collective-permute-start.2 = (f32[64,1]{1,0:T(8,128)S(1)}, f32[64,1]{1,0:T(8,128)S(1)}, u32[]{:S(2)}, u32[]{:S(2)}) collective-permute-start(f32[64,1]{1,0:T(8,128)S(1)} %get-tuple-element.5), channel_id=1, source_target_pairs={{0,4},{4,8},{8,12},{12,16},{16,20},{20,24},{24,28},{28,32},{32,36}... | collective-permute-start | bytes 776 | tf_op jit(solution)/shard_map/ppermute | solution.py:20
  68.3 6.4 %collective-permute-start = (f32[64,256]{1,0:T(8,128)S(1)}, f32[64,256]{1,0:T(8,128)S(1)}, u32[]{:S(2)}, u32[]{:S(2)}) collective-permute-start(f32[64,256]{1,0:T(8,128)S(1)} %bitcast.108), channel_id=1, source_target_pairs={{0,256},{256,0},{1,257},{257,1},{2,258},{258,2},{3,259},{259,3},{4... | collective-permute-start | bytes 196616 | tf_op jit(solution)/shard_map/ppermute | solution.py:54
  73.7 1.2 copy-start.3
  74.9 1.2 copy-start.4
  76.1 53.3 %copy-start.2 = (f32[64,4096]{1,0:T(8,128)}, f32[64,4096]{1,0:T(8,128)S(1)}, u32[]{:S(2)}) copy-start(f32[64,4096]{1,0:T(8,128)S(1)} %fusion.6) | copy-start | bytes 3145732
  99.7 17.1 %all-to-all-start.3 = ((f32[64,8,65]{2,1,0:T(8,128)}), f32[64,8,65]{2,1,0:T(8,128)S(1)}, u32[]{:S(2)}, u32[]{:S(2)}) async-start(f32[64,8,65]{2,1,0:T(8,128)} %pad_maximum_fusion.5), calls=%async_computation.3 | async-start | bytes 524288 | tf_op jit(solution)/shard_map/all_to_all | solution.py:42
  105.0 24.4 %collective-permute-start.4 = (f32[64,1]{1,0:T(8,128)}, f32[64,1]{1,0:T(8,128)S(1)}, u32[]{:S(2)}, u32[]{:S(2)}) collective-permute-start(f32[64,1]{1,0:T(8,128)} %get-tuple-element.2), channel_id=1, source_target_pairs={{4,0},{8,4},{12,8},{16,12},{20,16},{24,20},{28,24},{32,28},{36,32}... | collective-permute-start | bytes 776 | tf_op jit(solution)/shard_map/ppermute | solution.py:21
  106.3 23.1 %collective-permute-start.5 = (f32[64,1]{1,0:T(8,128)}, f32[64,1]{1,0:T(8,128)}, u32[]{:S(2)}, u32[]{:S(2)}) collective-permute-start(f32[64,1]{1,0:T(8,128)} %get-tuple-element.3), channel_id=1, source_target_pairs={{0,4},{4,8},{8,12},{12,16},{16,20},{20,24},{24,28},{28,32},{32,36}... | collective-permute-start | bytes 776 | tf_op jit(solution)/shard_map/ppermute | solution.py:20
  122.0 0.9 slice-start
  123.0 6.5 %collective-permute-start.3 = (f32[64,256]{1,0:T(8,128)S(1)}, f32[64,256]{1,0:T(8,128)S(1)}, u32[]{:S(2)}, u32[]{:S(2)}) collective-permute-start(f32[64,256]{1,0:T(8,128)S(1)} %bitcast.109), channel_id=1, source_target_pairs={{0,256},{256,0},{1,257},{257,1},{2,258},{258,2},{3,259},{259,3},{4... | collective-permute-start | bytes 196616 | tf_op jit(solution)/shard_map/ppermute | solution.py:54
where the time goes:
time: 132 us
  starting transfers between devices  47.9 us (36%)
  local copies, waits for them, and re-layouts  39.9 us (30%)
  other arithmetic  16.1 us (12%)
  waiting for transfers between devices  12.6 us (10%)
  blocking collectives  10.6 us (8%)
  matrix products  4.29 us (3%)
    scatter x2, local copies, waits for them, and re-layouts, body(): jnp.zeros((domains, width, rows), jnp.float32).at[owners, ranks]  23.1 us
    all_to_all x2, starting transfers between devices, sent_together(): lax.all_to_all(both, axis, split_axis=split_dim, concat_axis=concat_dim,...  20.9 us
    all_to_all x2, waiting for transfers between devices, sent_together(): lax.all_to_all(both, axis, split_axis=split_dim, concat_axis=concat_dim,...  12.6 us
    scatter x1, local copies, waits for them, and re-layouts, body(): slot_labels = jnp.full((domains, width), float(iface), jnp.float32).at[ow...  11.3 us
    ppermute x2, starting transfers between devices, swapped(): lax.ppermute(value, axis, [(i, i ^ 1 << stride) for i in range(lax.axis_s...  10.8 us
    all_to_all x1, blocking collectives, sum_at_owner(): lax.all_to_all(blocks, axis, split_axis=0, concat_axis=0, tiled=True)  10.6 us
    ppermute x2, starting transfers between devices, extended(): before = lax.ppermute(last, axis, up)  8.58 us
    scatter-add x2, other arithmetic, body(): jax.ops.segment_sum(got.reshape(-1, rows), target, num_segments=iface + 1)  7.01 us
  transfers between devices with their start and end apart: 9, of which 2 were waited for; matrix products, arithmetic and copies ran while one was open for 19% of the time, Pallas kernels for 0%

commit v1 on v0

v1 whole, which is shorter than its diff:
```python
import functools
import math

import jax
import jax.numpy as jnp
from jax import lax
from jax.experimental import pallas as pl
from jax.experimental.pallas import tpu as pltpu
from jax.sharding import PartitionSpec as P

MESH = pl.DeviceIdType.MESH
F32, BF16 = jnp.float32, jnp.bfloat16
LANES = 128
NT = (((1,), (1,)), ((), ()))


def halves(value):
    high = value.astype(BF16)
    return high, (value - high.astype(F32)).astype(BF16)


def iota(shape, dim):
    return lax.broadcasted_iota(jnp.int32, shape, dim).astype(F32)


def lanes_at(n, count):
    start = n * LANES
    return pl.ds(start if isinstance(n, int) else pl.multiple_of(start, LANES), count * LANES)


def dot(a, b):
    return jnp.dot(a, b, preferred_element_type=F32)


def kernel(
    ny, nz, nsub, field, previous, stiff, synth_t, owner, face, weight, latest, prior,
    state, older, newer, final, stiff_v, synth_v, owner_v, face_v, weight_v,
    part, part_in, packed, arrived, labels, labels_in,
    element, operator, pick, place, base,
    load_sem, part_send, part_recv, pack_send, pack_recv, halo_send, halo_recv, near_sem, out_sem,
):
    rows, points = older.shape
    tiles = points // LANES
    domains, height, _ = labels.shape
    iface = domains * height
    itiles = iface // LANES
    grp, mer, sub = lax.axis_index("grp"), lax.axis_index("mer"), lax.axis_index("sub")
    other = 1 - grp
    y, z = mer // nz, mer % nz
    above, below = (mer + 1) % domains, (mer + domains - 1) % domains

    barrier = pltpu.get_barrier_semaphore()

    def greet(sem, **where):
        pl.semaphore_signal(sem, inc=1, device_id=where, device_id_type=MESH)

    for k in range(1, nsub):
        greet(barrier, grp=grp, mer=mer, sub=(sub + k) % nsub)
    for k in range(1, nz):
        greet(barrier, grp=grp, mer=y * nz + (z + k) % nz, sub=sub)
    for k in range(ny):
        greet(barrier, grp=other, mer=(y + k) % ny * nz + z, sub=sub)
    greet(barrier, grp=grp, mer=above, sub=sub)
    greet(barrier, grp=grp, mer=below, sub=sub)

    def load(src, dst, n):
        copy = pltpu.make_async_copy(src, dst, load_sem.at[n])
        copy.start()
        return copy

    get_synth = load(synth_t.at[0], synth_v, 0)
    get_iface = load(field.at[0, :, pl.ds(0, iface)], state.at[:, pl.ds(LANES, iface)], 1)
    get_owner = load(owner, owner_v, 2)
    get_face = load(face, face_v, 3)
    get_weight = load(weight, weight_v, 4)
    get_stiff = load(stiff.at[0], stiff_v, 5)
    get_state = load(
        field.at[0, :, pl.ds(iface, points - iface)], state.at[:, pl.ds(LANES + iface, points - iface)], 6
    )
    get_older = load(previous.at[0], older, 7)

    def traces(value, step):
        high, low = halves(value)
        sums = dot(operator[...], jnp.concatenate([high, low, high, low], axis=0))
        part[step] = sums.reshape(nsub, rows, iface)

    def part_copy(step, k):
        to = (sub + k) % nsub
        return pltpu.make_async_remote_copy(
            src_ref=part.at[step, to],
            dst_ref=part_in.at[step, k - 1],
            send_sem=part_send.at[step, k - 1],
            recv_sem=part_recv.at[step, k - 1],
            device_id={"grp": grp, "mer": mer, "sub": to},
            device_id_type=MESH,
        )

    ways = sorted(range(1, nsub), key=lambda k: -min(k, nsub - k))

    get_synth.wait()
    high, low = halves(synth_v[...])
    high, low = high.astype(F32), low.astype(F32)
    operator[...] = jnp.concatenate([high, high, low, low], axis=0).T.astype(BF16)
    get_iface.wait()
    traces(state[:, LANES : LANES + iface], 0)

    pl.semaphore_wait(barrier, nsub - 1 + nz - 1 + ny + 2)
    for k in ways:
        part_copy(0, k).start()
    for k in range(ny):
        greet(near_sem, grp=other, mer=(y + k) % ny * nz + z, sub=sub)

    def halo_copy(src, dst, to, step, way):
        return pltpu.make_async_remote_copy(
            src_ref=src,
            dst_ref=dst,
            send_sem=halo_send.at[step, way],
            recv_sem=halo_recv.at[step, way],
            device_id={"grp": grp, "mer": to, "sub": sub},
            device_id_type=MESH,
        )

    def tile(ref, n, count=1):
        return ref.at[:, pl.ds(n * LANES, count * LANES)]

    up = [
        halo_copy(field.at[0, :, pl.ds(points - LANES, LANES)], tile(state, 0), above, 0, 0),
        halo_copy(tile(newer, tiles), tile(newer, 0), above, 1, 0),
    ]
    down = [
        halo_copy(field.at[0, :, pl.ds(0, LANES)], tile(state, tiles + 1), below, 0, 1),
        halo_copy(tile(newer, 1), tile(newer, tiles + 1), below, 1, 1),
    ]
    up[0].start()
    down[0].start()

    get_owner.wait()
    get_face.wait()
    get_weight.wait()
    own = owner_v[...].astype(F32)
    across = jnp.broadcast_to(own, (iface, iface))
    i, j = iota((iface, iface), 0), iota((iface, iface), 1)
    down_own = jnp.sum(jnp.where(i == j, across, 0.0), axis=1, keepdims=True)
    rank = jnp.sum(jnp.where((down_own == across) & (i < j), 1.0, 0.0), axis=0, keepdims=True)
    second = (rank >= height).astype(F32)
    row = own * height + rank - height * second
    hit = jnp.where(i == row, 1.0, 0.0)
    pick[0:iface, :] = (hit * (1.0 - second)).astype(BF16)
    pick[iface:, :] = (hit * second).astype(BF16)
    left_half = lax.broadcasted_iota(jnp.int32, (iface, LANES), 1) < LANES // 2
    names = jnp.broadcast_to(face_v[...].astype(F32), (LANES, iface)).astype(BF16)
    named = lax.dot_general(pick[...], names, NT, preferred_element_type=F32)
    labels[...] = jnp.where(left_half, named[:iface], named[iface:]).reshape(labels.shape)

    def owner_copy(src, dst, n, k):
        to = (y + ny // 2 + k // nz) % ny * nz + (z + nz // 2 + k % nz) % nz
        return pltpu.make_async_remote_copy(
            src_ref=src.at[to],
            dst_ref=dst.at[mer],
            send_sem=pack_send.at[n],
            recv_sem=pack_recv.at[n],
            device_id={"grp": other, "mer": to, "sub": sub},
            device_id_type=MESH,
        )

    def send_all(src, dst, n):
        def one(k, carry):
            owner_copy(src, dst, n, k).start()
            return carry

        lax.fori_loop(0, domains, one, 0, unroll=8)

    def all_of(src, dst, n):
        return pltpu.make_async_remote_copy(
            src_ref=src,
            dst_ref=dst,
            send_sem=pack_send.at[n],
            recv_sem=pack_recv.at[n],
            device_id={"grp": other, "mer": mer, "sub": sub},
            device_id_type=MESH,
        )

    pl.semaphore_wait(near_sem, ny)
    send_all(labels, labels_in, ITERS)

    def exchange(step):
        total = part[step, sub]
        for k in ways[::-1]:
            part_copy(step, k).wait_recv()
            total = total + part_in[step, k - 1]
        total = total * weight_v[...]
        high, low = halves(total)
        both = jnp.concatenate([high, low], axis=0)
        out = lax.dot_general(pick[...], both, NT, preferred_element_type=F32)
        out = out + pltpu.roll(out, LANES // 2, 1)
        packed[step] = jnp.where(left_half, out[:iface], out[iface:]).reshape(labels.shape)
        send_all(packed.at[step], arrived.at[step], step)

    exchange(0)

    get_stiff.wait()
    high, low = halves(stiff_v[...] * DT2)
    both = jnp.concatenate([high, low], axis=1)
    element[...] = jnp.concatenate([both, both], axis=0)
    lane = lax.broadcasted_iota(jnp.int32, (rows, LANES), 1)
    inner_low = jnp.where(mer > 0, 1.0, 0.0)
    inner_high = jnp.where(mer < domains - 1, 1.0, 0.0)

    def stepped(now, before, n, count, first=False, last=False):
        chunk = now[:, lanes_at(n, count + 2)]
        old = before(n, count)
        x = [chunk[:, LANES * c : LANES * (c + 1)] for c in range(count + 2)]
        if first:
            x[0] = x[0] * inner_low
        if last:
            x[-1] = x[-1] * inner_high
        high, low = halves(jnp.concatenate(x[1:-1], axis=0))
        product = dot(jnp.concatenate([high, low], axis=1), element[...])
        product = product[:, :LANES] + product[:, LANES:]
        right = [pltpu.roll(v, 1, 1) for v in x[:-1]]
        left = [pltpu.roll(v, LANES - 1, 1) for v in x[1:]]
        out = []
        for c in range(count):
            lower = jnp.where(lane == 0, right[c], right[c + 1])
            upper = jnp.where(lane == LANES - 1, left[c + 1], left[c])
            v = x[c + 1]
            lap = 2.0 * v - lower - upper
            out.append(
                2.0 * v - old[:, LANES * c : LANES * (c + 1)]
                - product[rows * c : rows * (c + 1)] - (DT2 * KAPPA) * lap
            )
        return jnp.concatenate(out, axis=1)

    def before_0(n, count):
        return older[:, lanes_at(n, count)]

    def before_1(n, count):
        return state[:, lanes_at(n + 1, count)]

    group = 4

    def run(now, before, out, shift, start, stop):
        whole = (stop - start) // group

        def one(g, carry):
            n = start + g * group
            out[:, lanes_at(n + shift, group)] = stepped(now, before, n, group)
            return carry

        lax.fori_loop(0, whole, one, 0)
        n, count = start + whole * group, stop - start - whole * group
        if count:
            out[:, lanes_at(n + shift, count)] = stepped(now, before, n, count)

    get_state.wait()
    get_older.wait()
    up[0].wait_recv()
    down[0].wait_recv()
    base[...] = stepped(state, before_0, 0, itiles, first=True)
    run(state, before_0, newer, 1, itiles, tiles - 1)
    newer[:, pl.ds(tiles * LANES, LANES)] = stepped(state, before_0, tiles - 1, 1, last=True)
    up[1].start()

    def put(src, dst, n):
        copy = pltpu.make_async_copy(src, dst, out_sem.at[n])
        copy.start()
        return copy

    puts = [put(tile(newer, 1 + itiles, tiles - itiles), tile(prior.at[0], itiles, tiles - itiles), 0)]
    all_of(labels, labels_in, ITERS).wait_recv()
    got = labels_in[...].reshape(iface, LANES)
    f = iota((iface, iface), 1)
    place[0:iface, :] = jnp.where(got[:, 0:1] == f, 1.0, 0.0).astype(BF16)
    half = LANES // 2
    place[iface:, :] = jnp.where(got[:, half : half + 1] == f, 1.0, 0.0).astype(BF16)
    run(newer, before_1, final, 0, itiles + 1, tiles - 1)
    puts.append(
        put(tile(final, itiles + 1, tiles - itiles - 2), tile(latest.at[0], itiles + 1, tiles - itiles - 2), 1)
    )

    def forced(step):
        all_of(packed.at[step], arrived.at[step], step).wait_recv()
        got = arrived[step].reshape(iface, LANES).T
        high, low = halves(got)
        both = jnp.concatenate(
            [jnp.concatenate([v[:half], v[half:]], axis=1) for v in (high, low)], axis=0
        )
        out = dot(both, place[...])
        return base[...] + DT2 * (out[:rows] + out[rows:])

    mid = forced(0)
    newer[:, pl.ds(LANES, iface)] = mid
    traces(mid, 1)
    for k in ways:
        part_copy(1, k).start()
    down[1].start()
    puts.append(put(tile(newer, 1, itiles), tile(prior.at[0], 0, itiles), 2))

    up[1].wait_recv()
    ahead = stepped(newer, before_1, 0, itiles + 1, first=True)
    base[...] = ahead[:, :iface]
    final[:, pl.ds(iface, LANES)] = ahead[:, iface:]
    puts.append(put(tile(final, itiles), tile(latest.at[0], itiles), 3))

    exchange(1)
    down[1].wait_recv()
    final[:, pl.ds((tiles - 1) * LANES, LANES)] = stepped(newer, before_1, tiles - 1, 1, last=True)
    puts.append(put(tile(final, tiles - 1), tile(latest.at[0], tiles - 1), 4))

    final[:, pl.ds(0, iface)] = forced(1)
    puts.append(put(tile(final, 0, itiles), tile(latest.at[0], 0, itiles), 5))
    for step in range(ITERS):
        for k in ways:
            part_copy(step, k).wait_send()
        all_of(packed.at[step], arrived.at[step], step).wait_send()
        up[step].wait_send()
        down[step].wait_send()
    all_of(labels, labels_in, ITERS).wait_send()
    for copy in puts:
        copy.wait()


ITERS = 2
DT2 = 0.5
KAPPA = 0.5


def body(mesh_shape, field, previous, stiff, synth, owner, face, weight):
    domains, nsub = mesh_shape["mer"], mesh_shape["sub"]
    nz = 1 << (int(math.log2(domains)) // 2)
    ny = domains // nz
    _, rows, points = field.shape
    iface = owner.shape[1]
    height = iface // domains
    edge = stiff.shape[1]
    dma = pltpu.SemaphoreType.DMA
    any_space = pl.BlockSpec(memory_space=pl.ANY)
    blocks = (domains, height, LANES)
    scratch = [
        pltpu.VMEM((rows, points + 2 * LANES), F32),
        pltpu.VMEM((rows, points), F32),
        pltpu.VMEM((rows, points + 2 * LANES), F32),
        pltpu.VMEM((rows, points), F32),
        pltpu.VMEM((edge, edge), F32),
        pltpu.VMEM((rows, nsub * rows), F32),
        pltpu.VMEM((1, iface), jnp.int32),
        pltpu.VMEM((1, iface), jnp.int32),
        pltpu.VMEM((1, iface), F32),
        pltpu.VMEM((ITERS, nsub, rows, iface), F32),
        pltpu.VMEM((ITERS, nsub - 1, rows, iface), F32),
        pltpu.VMEM((ITERS, *blocks), F32),
        pltpu.VMEM((ITERS, *blocks), F32),
        pltpu.VMEM(blocks, F32),
        pltpu.VMEM(blocks, F32),
        pltpu.VMEM((2 * edge, 2 * edge), BF16),
        pltpu.VMEM((nsub * rows, 4 * rows), BF16),
        pltpu.VMEM((2 * iface, iface), BF16),
        pltpu.VMEM((2 * iface, iface), BF16),
        pltpu.VMEM((rows, iface), F32),
        dma((8,)),
        dma((ITERS, nsub - 1)),
        dma((ITERS, nsub - 1)),
        dma((ITERS + 1,)),
        dma((ITERS + 1,)),
        dma((ITERS, 2)),
        dma((ITERS, 2)),
        pltpu.SemaphoreType.REGULAR,
        dma((6,)),
    ]
    out = jax.ShapeDtypeStruct(field.shape, F32)
    return pl.pallas_call(
        functools.partial(kernel, ny, nz, nsub),
        out_shape=(out, out),
        in_specs=[any_space] * 7,
        out_specs=(any_space, any_space),
        scratch_shapes=scratch,
        compiler_params=pltpu.CompilerParams(
            collective_id=0, has_side_effects=True, vmem_limit_bytes=40 << 20
        ),
    )(
        field, previous, stiff, jnp.swapaxes(synth, 1, 2), owner.reshape(1, iface), face, weight
    )


def solution(mesh):
    in_specs = (
        P("grp", "sub", "mer"),
        P("grp", "sub", "mer"),
        P("grp", None, None),
        P("grp", None, "sub"),
        P("grp", "mer", None),
        P("grp", "mer"),
        P("grp", "mer"),
    )
    out_specs = (P("grp", "sub", "mer"), P("grp", "sub", "mer"))
    return jax.shard_map(
        functools.partial(body, dict(mesh.shape)),
        mesh=mesh,
        in_specs=in_specs,
        out_specs=out_specs,
        check_vma=False,
    )
```

time: 132 us -> 50.1 us (0.38)
  starting transfers between devices: 47.9 us -> 0 us
  Pallas kernels: 0 us -> 42.4 us
  local copies, waits for them, and re-layouts: 39.9 us -> 6.76 us
  other arithmetic: 16.1 us -> 0 us
  waiting for transfers between devices: 12.6 us -> 0 us
  blocking collectives: 10.6 us -> 0 us
  matrix products: 4.29 us -> 0 us
    pallas_call x0 -> x1, Pallas kernels: none -> 42.4 us  [body(): pl.pallas_call(functools.partial(kernel, ny, nz, nsub), out_shape=(out, o...]
    scatter x3 -> x0, local copies, waits for them, and re-layouts: 34.4 us -> none  [the longest x2 23.1 us: body(): jnp.zeros((domains, width, rows), jnp.float32).at[owners, ranks]]
    all_to_all x3 -> x0, starting transfers between devices: 25.9 us -> none  [the longest x2 20.9 us: sent_together(): lax.all_to_all(both, axis, split_axis=split_dim, concat_axis=concat_dim,...]
    ppermute x6 -> x0, starting transfers between devices: 22 us -> none  [the longest x2 10.8 us: swapped(): lax.ppermute(value, axis, [(i, i ^ 1 << stride) for i in range(lax.axis_s...]
    all_to_all x3 -> x0, waiting for transfers between devices: 12.6 us -> none  [the longest x2 12.6 us: sent_together(): lax.all_to_all(both, axis, split_axis=split_dim, concat_axis=concat_dim,...]
    all_to_all x1 -> x0, blocking collectives: 10.6 us -> none  [sum_at_owner(): lax.all_to_all(blocks, axis, split_axis=0, concat_axis=0, tiled=True)]
    scatter-add x2 -> x0, other arithmetic: 7.01 us -> none  [body(): jax.ops.segment_sum(got.reshape(-1, rows), target, num_segments=iface + 1)]
    unnamed x20 -> x16, local copies, waits for them, and re-layouts: 2.11 us -> 6.76 us
  transfers between devices with their start and end apart: 9 -> 0, of which waited for: 2 -> 0; matrix products, arithmetic and copies ran while one was open for 19% -> 0% of each run, Pallas kernels for 0% -> 0%
where the time goes in v1:
time: 50.1 us; the launch traced here: 49.8 us
  Pallas kernels  42.4 us (85%)
  local copies, waits for them, and re-layouts  6.76 us (13%)
  between operations  0.67 us (1%)
    pallas_call x1, Pallas kernels, body(): pl.pallas_call(functools.partial(kernel, ny, nz, nsub), out_shape=(out, o...  42.4 us
    unnamed x16, local copies, waits for them, and re-layouts  6.76 us

profile of v1, /device:TPU:1, one launch (start us, length us, event | category | flops | bytes accessed | tf_op | source)
XLA Modules:
  0.0 49.8 jit_solution(6054152962399900973)
XLA Ops:
  0.6 0.0 copy-start.5
  0.6 0.0 copy-start.6
  0.7 0.0 copy-start.4
  0.7 0.7 %copy-done.5 = s32[1,256]{1,0:T(1,128)S(1)} copy-done((s32[1,256]{1,0:T(1,128)S(1)}, s32[1,256]{1,0:T(1,128)}, u32[]{:S(2)}) %copy-start.5) | copy-done | bytes 1048
  1.3 0.0 copy-done.6
  1.3 0.0 copy-done.4
  1.3 0.0 copy-start
  1.3 1.2 %copy-done = f32[1,64,4096]{2,1,0:T(8,128)S(1)} copy-done((f32[1,64,4096]{2,1,0:T(8,128)S(1)}, f32[1,64,4096]{2,1,0:T(8,128)}, u32[]{:S(2)}) %copy-start) | copy-done | bytes 1048600
  2.6 0.0 copy-start.1
  2.6 1.2 %copy-done.1 = f32[1,64,4096]{2,1,0:T(8,128)S(1)} copy-done((f32[1,64,4096]{2,1,0:T(8,128)S(1)}, f32[1,64,4096]{2,1,0:T(8,128)}, u32[]{:S(2)}) %copy-start.1) | copy-done | bytes 1048600
  3.8 0.0 copy-start.2
  3.8 0.8 %copy-done.2 = f32[1,128,128]{2,1,0:T(8,128)S(1)} copy-done((f32[1,128,128]{2,1,0:T(8,128)S(1)}, f32[1,128,128]{2,1,0:T(8,128)}, u32[]{:S(2)}) %copy-start.2) | copy-done | bytes 65560
  4.6 0.0 copy-start.3
  4.6 0.8 %copy-done.3 = f32[1,256,64]{1,2,0:T(8,128)S(1)} copy-done((f32[1,256,64]{1,2,0:T(8,128)S(1)}, f32[1,256,64]{1,2,0:T(8,128)}, u32[]{:S(2)}) %copy-start.3) | copy-done | bytes 65560
  5.5 42.4 %shard_map.86 = (f32[1,64,4096]{2,1,0:T(8,128)S(1)}, f32[1,64,4096]{2,1,0:T(8,128)S(1)}) custom-call(f32[1,64,4096]{2,1,0:T(8,128)S(1)} %copy-done, f32[1,64,4096]{2,1,0:T(8,128)S(1)} %copy-done.1, f32[1,128,128]{2,1,0:T(8,128)S(1)} %copy-done.2, f32[1,64,256]{2,1,0:T(8,128)S(1)} %bitcast.2, s32[1,256]{1,0:T(1,128)S(1)} %bitcast.3, s32[1,256]{1,0:T(1,128)S(1)} %copy-done.5, ...), custom_call_target="tpu_custom_call" | custom-call | tf_op jit(solution)/shard_map/pallas_call | solution.py:371
  47.8 1.0 %copy.11 = f32[1,64,4096]{2,1,0:T(8,128)} copy(f32[1,64,4096]{2,1,0:T(8,128)S(1)} %get-tuple-element.4) | data formatting | bytes 2097152
  48.8 1.0 %copy.12 = f32[1,64,4096]{2,1,0:T(8,128)} copy(f32[1,64,4096]{2,1,0:T(8,128)S(1)} %get-tuple-element.5) | data formatting | bytes 2097152
Async XLA Ops:
  0.6 0.7 %copy-start.5 = (s32[1,256]{1,0:T(1,128)S(1)}, s32[1,256]{1,0:T(1,128)}, u32[]{:S(2)}) copy-start(s32[1,256]{1,0:T(1,128)} %face.1) | copy-start | bytes 3076
  0.6 0.7 %copy-start.6 = (f32[1,256]{1,0:T(1,128)S(1)}, f32[1,256]{1,0:T(1,128)}, u32[]{:S(2)}) copy-start(f32[1,256]{1,0:T(1,128)} %weight.1) | copy-start | bytes 3076
  0.7 0.7 %copy-start.4 = (s32[1,256,1]{1,2,0:T(1,128)S(1)}, s32[1,256,1]{1,2,0:T(1,128)}, u32[]{:S(2)}) copy-start(s32[1,256,1]{1,2,0:T(1,128)} %param.11) | copy-start | bytes 3076
  1.3 1.2 %copy-start = (f32[1,64,4096]{2,1,0:T(8,128)S(1)}, f32[1,64,4096]{2,1,0:T(8,128)}, u32[]{:S(2)}) copy-start(f32[1,64,4096]{2,1,0:T(8,128)} %field.1) | copy-start | bytes 3145732
  2.6 1.2 %copy-start.1 = (f32[1,64,4096]{2,1,0:T(8,128)S(1)}, f32[1,64,4096]{2,1,0:T(8,128)}, u32[]{:S(2)}) copy-start(f32[1,64,4096]{2,1,0:T(8,128)} %previous.1) | copy-start | bytes 3145732
  3.8 0.8 %copy-start.2 = (f32[1,128,128]{2,1,0:T(8,128)S(1)}, f32[1,128,128]{2,1,0:T(8,128)}, u32[]{:S(2)}) copy-start(f32[1,128,128]{2,1,0:T(8,128)} %stiff.1) | copy-start | bytes 196612
  4.6 0.8 %copy-start.3 = (f32[1,256,64]{1,2,0:T(8,128)S(1)}, f32[1,256,64]{1,2,0:T(8,128)}, u32[]{:S(2)}) copy-start(f32[1,256,64]{1,2,0:T(8,128)} %param.10) | copy-start | bytes 196612

commit v2 on v1

--- a/solution.py
+++ b/solution.py
@@ -33,11 +33,11 @@
 
 
 def kernel(
-    ny, nz, nsub, field, previous, stiff, synth_t, owner, face, weight, latest, prior,
-    state, older, newer, final, stiff_v, synth_v, owner_v, face_v, weight_v,
+    ny, nz, nsub, field, previous, stiff, synth_t, owner, face, weight, final, newer,
+    state, older, halo, stiff_v, synth_v, owner_v, face_v, weight_v,
     part, part_in, packed, arrived, labels, labels_in,
     element, operator, pick, place, base,
-    load_sem, part_send, part_recv, pack_send, pack_recv, halo_send, halo_recv, near_sem, out_sem,
+    load_sem, part_send, part_recv, pack_send, pack_recv, halo_send, halo_recv, near_sem,
 ):
     rows, points = older.shape
     tiles = points // LANES
@@ -69,13 +69,13 @@
         return copy
 
     get_synth = load(synth_t.at[0], synth_v, 0)
-    get_iface = load(field.at[0, :, pl.ds(0, iface)], state.at[:, pl.ds(LANES, iface)], 1)
+    get_iface = load(field.at[0, :, pl.ds(0, iface)], state.at[:, pl.ds(0, iface)], 1)
     get_owner = load(owner, owner_v, 2)
     get_face = load(face, face_v, 3)
     get_weight = load(weight, weight_v, 4)
     get_stiff = load(stiff.at[0], stiff_v, 5)
     get_state = load(
-        field.at[0, :, pl.ds(iface, points - iface)], state.at[:, pl.ds(LANES + iface, points - iface)], 6
+        field.at[0, :, pl.ds(iface, points - iface)], state.at[:, pl.ds(iface, points - iface)], 6
     )
     get_older = load(previous.at[0], older, 7)
 
@@ -102,7 +102,7 @@
     high, low = high.astype(F32), low.astype(F32)
     operator[...] = jnp.concatenate([high, high, low, low], axis=0).T.astype(BF16)
     get_iface.wait()
-    traces(state[:, LANES : LANES + iface], 0)
+    traces(state[:, :iface], 0)
 
     pl.semaphore_wait(barrier, nsub - 1 + nz - 1 + ny + 2)
     for k in ways:
@@ -120,16 +120,16 @@
             device_id_type=MESH,
         )
 
-    def tile(ref, n, count=1):
-        return ref.at[:, pl.ds(n * LANES, count * LANES)]
+    def lanes_of(ref, n):
+        return ref.at[:, pl.ds(n * LANES, LANES)]
 
     up = [
-        halo_copy(field.at[0, :, pl.ds(points - LANES, LANES)], tile(state, 0), above, 0, 0),
-        halo_copy(tile(newer, tiles), tile(newer, 0), above, 1, 0),
+        halo_copy(lanes_of(field.at[0], tiles - 1), halo.at[0, 0], above, 0, 0),
+        halo_copy(lanes_of(newer, tiles - 1), halo.at[1, 0], above, 1, 0),
     ]
     down = [
-        halo_copy(field.at[0, :, pl.ds(0, LANES)], tile(state, tiles + 1), below, 0, 1),
-        halo_copy(tile(newer, 1), tile(newer, tiles + 1), below, 1, 1),
+        halo_copy(lanes_of(field.at[0], 0), halo.at[0, 1], below, 0, 1),
+        halo_copy(lanes_of(newer, 0), halo.at[1, 1], below, 1, 1),
     ]
     up[0].start()
     down[0].start()
@@ -206,14 +206,17 @@
     inner_low = jnp.where(mer > 0, 1.0, 0.0)
     inner_high = jnp.where(mer < domains - 1, 1.0, 0.0)
 
-    def stepped(now, before, n, count, first=False, last=False):
-        chunk = now[:, lanes_at(n, count + 2)]
-        old = before(n, count)
-        x = [chunk[:, LANES * c : LANES * (c + 1)] for c in range(count + 2)]
+    def stepped(step, n, count):
+        now, before = ((state, older), (newer, state))[step]
+        static = isinstance(n, int)
+        first, last = static and n == 0, static and n + count == tiles
+        chunk = now[:, lanes_at(n if first else n - 1, count + 2 - first - last)]
+        x = [chunk[:, LANES * c : LANES * (c + 1)] for c in range(chunk.shape[1] // LANES)]
         if first:
-            x[0] = x[0] * inner_low
+            x = [halo[step, 0] * inner_low] + x
         if last:
-            x[-1] = x[-1] * inner_high
+            x = x + [halo[step, 1] * inner_high]
+        old = before[:, lanes_at(n, count)]
         high, low = halves(jnp.concatenate(x[1:-1], axis=0))
         product = dot(jnp.concatenate([high, low], axis=1), element[...])
         product = product[:, :LANES] + product[:, LANES:]
@@ -231,52 +234,37 @@
             )
         return jnp.concatenate(out, axis=1)
 
-    def before_0(n, count):
-        return older[:, lanes_at(n, count)]
-
-    def before_1(n, count):
-        return state[:, lanes_at(n + 1, count)]
-
     group = 4
 
-    def run(now, before, out, shift, start, stop):
+    def run(step, out, start, stop):
         whole = (stop - start) // group
 
         def one(g, carry):
             n = start + g * group
-            out[:, lanes_at(n + shift, group)] = stepped(now, before, n, group)
+            out[:, lanes_at(n, group)] = stepped(step, n, group)
             return carry
 
         lax.fori_loop(0, whole, one, 0)
         n, count = start + whole * group, stop - start - whole * group
         if count:
-            out[:, lanes_at(n + shift, count)] = stepped(now, before, n, count)
+            out[:, lanes_at(n, count)] = stepped(step, n, count)
 
     get_state.wait()
     get_older.wait()
     up[0].wait_recv()
     down[0].wait_recv()
-    base[...] = stepped(state, before_0, 0, itiles, first=True)
-    run(state, before_0, newer, 1, itiles, tiles - 1)
-    newer[:, pl.ds(tiles * LANES, LANES)] = stepped(state, before_0, tiles - 1, 1, last=True)
+    base[...] = stepped(0, 0, itiles)
+    run(0, newer, itiles, tiles - 1)
+    newer[:, pl.ds((tiles - 1) * LANES, LANES)] = stepped(0, tiles - 1, 1)
     up[1].start()
 
-    def put(src, dst, n):
-        copy = pltpu.make_async_copy(src, dst, out_sem.at[n])
-        copy.start()
-        return copy
-
-    puts = [put(tile(newer, 1 + itiles, tiles - itiles), tile(prior.at[0], itiles, tiles - itiles), 0)]
     all_of(labels, labels_in, ITERS).wait_recv()
     got = labels_in[...].reshape(iface, LANES)
     f = iota((iface, iface), 1)
     place[0:iface, :] = jnp.where(got[:, 0:1] == f, 1.0, 0.0).astype(BF16)
     half = LANES // 2
     place[iface:, :] = jnp.where(got[:, half : half + 1] == f, 1.0, 0.0).astype(BF16)
-    run(newer, before_1, final, 0, itiles + 1, tiles - 1)
-    puts.append(
-        put(tile(final, itiles + 1, tiles - itiles - 2), tile(latest.at[0], itiles + 1, tiles - itiles - 2), 1)
-    )
+    run(1, final, itiles + 1, tiles - 1)
 
     def forced(step):
         all_of(packed.at[step], arrived.at[step], step).wait_recv()
@@ -289,26 +277,22 @@
         return base[...] + DT2 * (out[:rows] + out[rows:])
 
     mid = forced(0)
-    newer[:, pl.ds(LANES, iface)] = mid
+    newer[:, pl.ds(0, iface)] = mid
     traces(mid, 1)
     for k in ways:
         part_copy(1, k).start()
     down[1].start()
-    puts.append(put(tile(newer, 1, itiles), tile(prior.at[0], 0, itiles), 2))
 
     up[1].wait_recv()
-    ahead = stepped(newer, before_1, 0, itiles + 1, first=True)
+    ahead = stepped(1, 0, itiles + 1)
     base[...] = ahead[:, :iface]
     final[:, pl.ds(iface, LANES)] = ahead[:, iface:]
-    puts.append(put(tile(final, itiles), tile(latest.at[0], itiles), 3))
 
     exchange(1)
     down[1].wait_recv()
-    final[:, pl.ds((tiles - 1) * LANES, LANES)] = stepped(newer, before_1, tiles - 1, 1, last=True)
-    puts.append(put(tile(final, tiles - 1), tile(latest.at[0], tiles - 1), 4))
+    final[:, pl.ds((tiles - 1) * LANES, LANES)] = stepped(1, tiles - 1, 1)
 
     final[:, pl.ds(0, iface)] = forced(1)
-    puts.append(put(tile(final, 0, itiles), tile(latest.at[0], 0, itiles), 5))
     for step in range(ITERS):
         for k in ways:
             part_copy(step, k).wait_send()
@@ -316,13 +300,22 @@
         up[step].wait_send()
         down[step].wait_send()
     all_of(labels, labels_in, ITERS).wait_send()
-    for copy in puts:
+
+def written(final, newer, latest, prior, sem):
+    copies = [
+        pltpu.make_async_copy(src, dst.at[0], sem.at[n])
+        for n, (src, dst) in enumerate(((final, latest), (newer, prior)))
+    ]
+    for copy in copies:
+        copy.start()
+    for copy in copies:
         copy.wait()
 
 
 ITERS = 2
 DT2 = 0.5
 KAPPA = 0.5
+RESERVED = 64900000
 
 
 def body(mesh_shape, field, previous, stiff, synth, owner, face, weight):
@@ -334,13 +327,13 @@
     height = iface // domains
     edge = stiff.shape[1]
     dma = pltpu.SemaphoreType.DMA
-    any_space = pl.BlockSpec(memory_space=pl.ANY)
+    anywhere = pl.BlockSpec(memory_space=pl.ANY)
+    vmem = pl.BlockSpec(memory_space=pltpu.VMEM)
     blocks = (domains, height, LANES)
     scratch = [
-        pltpu.VMEM((rows, points + 2 * LANES), F32),
         pltpu.VMEM((rows, points), F32),
-        pltpu.VMEM((rows, points + 2 * LANES), F32),
         pltpu.VMEM((rows, points), F32),
+        pltpu.VMEM((ITERS, 2, rows, LANES), F32),
         pltpu.VMEM((edge, edge), F32),
         pltpu.VMEM((rows, nsub * rows), F32),
         pltpu.VMEM((1, iface), jnp.int32),
@@ -365,21 +358,28 @@
         dma((ITERS, 2)),
         dma((ITERS, 2)),
         pltpu.SemaphoreType.REGULAR,
-        dma((6,)),
     ]
-    out = jax.ShapeDtypeStruct(field.shape, F32)
-    return pl.pallas_call(
+    stepped = pl.pallas_call(
         functools.partial(kernel, ny, nz, nsub),
-        out_shape=(out, out),
-        in_specs=[any_space] * 7,
-        out_specs=(any_space, any_space),
+        out_shape=(pltpu.VMEM((rows, points), F32),) * 2,
+        in_specs=[anywhere] * 7,
+        out_specs=(vmem, vmem),
         scratch_shapes=scratch,
         compiler_params=pltpu.CompilerParams(
-            collective_id=0, has_side_effects=True, vmem_limit_bytes=40 << 20
+            collective_id=0, has_side_effects=True, vmem_limit_bytes=RESERVED
         ),
     )(
         field, previous, stiff, jnp.swapaxes(synth, 1, 2), owner.reshape(1, iface), face, weight
     )
+    out = jax.ShapeDtypeStruct(field.shape, F32)
+    return pl.pallas_call(
+        written,
+        out_shape=(out, out),
+        in_specs=[anywhere] * 2,
+        out_specs=(anywhere, anywhere),
+        scratch_shapes=[dma((2,))],
+        compiler_params=pltpu.CompilerParams(vmem_limit_bytes=1 << 20),
+    )(*stepped)
 
 
 def solution(mesh):

time: 50.1 us -> 44.5 us (0.89)
  local copies, waits for them, and re-layouts: 6.76 us -> 0 us
  Pallas kernels: 42.4 us -> 43.7 us
    unnamed x16 -> x0, local copies, waits for them, and re-layouts: 6.76 us -> none
    pallas_call x1 -> x2, Pallas kernels: 42.4 us -> 43.7 us  [the longest x1 42.4 us: body(): pl.pallas_call(functools.partial(kernel, ny, nz, nsub), out_shape=(pltpu....]
where the time goes in v2:
time: 44.5 us; the launch traced here: 44.4 us
  Pallas kernels  43.7 us (98%)
  between operations  0.64 us (1%)
    pallas_call x1, Pallas kernels, body(): pl.pallas_call(functools.partial(kernel, ny, nz, nsub), out_shape=(pltpu....  42.4 us
    pallas_call x1, Pallas kernels, body(): pl.pallas_call(written, out_shape=(out, out), in_specs=[anywhere] * 2, ou...  1.33 us

profile of v2, /device:TPU:1, one launch (start us, length us, event | category | flops | bytes accessed | tf_op | source)
XLA Modules:
  0.0 44.4 jit_solution(5947834194085089306)
XLA Ops:
  0.6 42.4 %shard_map.86 = (f32[64,4096]{1,0:T(8,128)S(1)}, f32[64,4096]{1,0:T(8,128)S(1)}) custom-call(f32[1,64,4096]{2,1,0:T(8,128)} %field.1, f32[1,64,4096]{2,1,0:T(8,128)} %previous.1, f32[1,128,128]{2,1,0:T(8,128)} %stiff.1, f32[1,64,256]{2,1,0:T(8,128)} %bitcast.2, s32[1,256]{1,0:T(1,128)} %bitcast.3, s32[1,256]{1,0:T(1,128)} %face.1, f32[1,256]{1,0:T(1,128)} %weight.1), custom_call_target="tpu_custom_call" | custom-call | tf_op jit(solution)/shard_map/pallas_call | solution.py:362
  43.0 1.3 %shard_map.87 = (f32[1,64,4096]{2,1,0:T(8,128)}, f32[1,64,4096]{2,1,0:T(8,128)}) custom-call(f32[64,4096]{1,0:T(8,128)S(1)} %get-tuple-element.4.final, f32[64,4096]{1,0:T(8,128)S(1)} %get-tuple-element.5.newer), custom_call_target="tpu_custom_call" | custom-call | tf_op jit(solution)/shard_map/pallas_call | solution.py:375

commit v3 on v2

--- a/solution.py
+++ b/solution.py
@@ -35,13 +35,13 @@
 def kernel(
     ny, nz, nsub, field, previous, stiff, synth_t, owner, face, weight, final, newer,
     state, older, halo, stiff_v, synth_v, owner_v, face_v, weight_v,
-    part, part_in, packed, arrived, labels, labels_in,
+    part, part_in, first, first_in, second, second_in,
     element, operator, pick, place, base,
     load_sem, part_send, part_recv, pack_send, pack_recv, halo_send, halo_recv, near_sem,
 ):
     rows, points = older.shape
     tiles = points // LANES
-    domains, height, _ = labels.shape
+    domains, height, _ = second.shape
     iface = domains * height
     itiles = iface // LANES
     grp, mer, sub = lax.axis_index("grp"), lax.axis_index("mer"), lax.axis_index("sub")
@@ -53,15 +53,6 @@
 
     def greet(sem, **where):
         pl.semaphore_signal(sem, inc=1, device_id=where, device_id_type=MESH)
-
-    for k in range(1, nsub):
-        greet(barrier, grp=grp, mer=mer, sub=(sub + k) % nsub)
-    for k in range(1, nz):
-        greet(barrier, grp=grp, mer=y * nz + (z + k) % nz, sub=sub)
-    for k in range(ny):
-        greet(barrier, grp=other, mer=(y + k) % ny * nz + z, sub=sub)
-    greet(barrier, grp=grp, mer=above, sub=sub)
-    greet(barrier, grp=grp, mer=below, sub=sub)
 
     def load(src, dst, n):
         copy = pltpu.make_async_copy(src, dst, load_sem.at[n])
@@ -79,6 +70,15 @@
     )
     get_older = load(previous.at[0], older, 7)
 
+    for k in range(1, nsub):
+        greet(barrier, grp=grp, mer=mer, sub=(sub + k) % nsub)
+    for k in range(1, nz):
+        greet(barrier, grp=grp, mer=y * nz + (z + k) % nz, sub=sub)
+    for k in range(ny):
+        greet(barrier, grp=other, mer=(y + k) % ny * nz + z, sub=sub)
+    greet(barrier, grp=grp, mer=above, sub=sub)
+    greet(barrier, grp=grp, mer=below, sub=sub)
+
     def traces(value, step):
         high, low = halves(value)
         sums = dot(operator[...], jnp.concatenate([high, low, high, low], axis=0))
@@ -142,46 +142,45 @@
     i, j = iota((iface, iface), 0), iota((iface, iface), 1)
     down_own = jnp.sum(jnp.where(i == j, across, 0.0), axis=1, keepdims=True)
     rank = jnp.sum(jnp.where((down_own == across) & (i < j), 1.0, 0.0), axis=0, keepdims=True)
-    second = (rank >= height).astype(F32)
-    row = own * height + rank - height * second
+    late = (rank >= height).astype(F32)
+    row = own * height + rank - height * late
     hit = jnp.where(i == row, 1.0, 0.0)
-    pick[0:iface, :] = (hit * (1.0 - second)).astype(BF16)
-    pick[iface:, :] = (hit * second).astype(BF16)
+    pick[0:iface, :] = (hit * (1.0 - late)).astype(BF16)
+    pick[iface:, :] = (hit * late).astype(BF16)
     left_half = lax.broadcasted_iota(jnp.int32, (iface, LANES), 1) < LANES // 2
-    names = jnp.broadcast_to(face_v[...].astype(F32), (LANES, iface)).astype(BF16)
-    named = lax.dot_general(pick[...], names, NT, preferred_element_type=F32)
-    labels[...] = jnp.where(left_half, named[:iface], named[iface:]).reshape(labels.shape)
-
-    def owner_copy(src, dst, n, k):
-        to = (y + ny // 2 + k // nz) % ny * nz + (z + nz // 2 + k % nz) % nz
+
+    named = jnp.where(iota((LANES, iface), 0) == rank, face_v[...].astype(F32), 0.0).astype(BF16)
+    chosen = jnp.where(iota((domains, iface), 0) == own, 1.0, 0.0).astype(BF16)
+    names = lax.dot_general(chosen, named, NT, preferred_element_type=F32)
+    first[:, pl.ds(height, 1), :] = names.reshape(domains, 1, LANES)
+
+    offsets = [(a, b) for a in range(ny) for b in range(nz)]
+    offsets.sort(key=lambda o: -(min(o[0], ny - o[0]) + min(o[1], nz - o[1])))
+    y_at = [(y + a) % ny * nz for a in range(ny)]
+    z_at = [(z + b) % nz for b in range(nz)]
+    sent, landed = (first, second), (first_in, second_in)
+
+    def send_all(step):
+        for a, b in offsets:
+            to = y_at[a] + z_at[b]
+            pltpu.make_async_remote_copy(
+                src_ref=sent[step].at[to],
+                dst_ref=landed[step].at[mer],
+                send_sem=pack_send.at[step],
+                recv_sem=pack_recv.at[step],
+                device_id={"grp": other, "mer": to, "sub": sub},
+                device_id_type=MESH,
+            ).start()
+
+    def all_of(step):
         return pltpu.make_async_remote_copy(
-            src_ref=src.at[to],
-            dst_ref=dst.at[mer],
-            send_sem=pack_send.at[n],
-            recv_sem=pack_recv.at[n],
-            device_id={"grp": other, "mer": to, "sub": sub},
-            device_id_type=MESH,
-        )
-
-    def send_all(src, dst, n):
-        def one(k, carry):
-            owner_copy(src, dst, n, k).start()
-            return carry
-
-        lax.fori_loop(0, domains, one, 0, unroll=8)
-
-    def all_of(src, dst, n):
-        return pltpu.make_async_remote_copy(
-            src_ref=src,
-            dst_ref=dst,
-            send_sem=pack_send.at[n],
-            recv_sem=pack_recv.at[n],
+            src_ref=sent[step],
+            dst_ref=landed[step],
+            send_sem=pack_send.at[step],
+            recv_sem=pack_recv.at[step],
             device_id={"grp": other, "mer": mer, "sub": sub},
             device_id_type=MESH,
         )
-
-    pl.semaphore_wait(near_sem, ny)
-    send_all(labels, labels_in, ITERS)
 
     def exchange(step):
         total = part[step, sub]
@@ -193,8 +192,11 @@
         both = jnp.concatenate([high, low], axis=0)
         out = lax.dot_general(pick[...], both, NT, preferred_element_type=F32)
         out = out + pltpu.roll(out, LANES // 2, 1)
-        packed[step] = jnp.where(left_half, out[:iface], out[iface:]).reshape(labels.shape)
-        send_all(packed.at[step], arrived.at[step], step)
+        out = jnp.where(left_half, out[:iface], out[iface:])
+        sent[step][:, pl.ds(0, height), :] = out.reshape(domains, height, LANES)
+        if step == 0:
+            pl.semaphore_wait(near_sem, ny)
+        send_all(step)
 
     exchange(0)
 
@@ -258,17 +260,27 @@
     newer[:, pl.ds((tiles - 1) * LANES, LANES)] = stepped(0, tiles - 1, 1)
     up[1].start()
 
-    all_of(labels, labels_in, ITERS).wait_recv()
-    got = labels_in[...].reshape(iface, LANES)
-    f = iota((iface, iface), 1)
-    place[0:iface, :] = jnp.where(got[:, 0:1] == f, 1.0, 0.0).astype(BF16)
+    run(1, final, itiles + 1, tiles - 1)
+
     half = LANES // 2
-    place[iface:, :] = jnp.where(got[:, half : half + 1] == f, 1.0, 0.0).astype(BF16)
-    run(1, final, itiles + 1, tiles - 1)
+    block = lax.broadcasted_iota(jnp.int32, (iface, domains), 0) // height
+    spread = jnp.where(block == lax.broadcasted_iota(jnp.int32, (iface, domains), 1), 1.0, 0.0).astype(BF16)
+    slot = lax.broadcasted_iota(jnp.int32, (iface, LANES), 1)
+    slot = slot - lax.broadcasted_iota(jnp.int32, (iface, LANES), 0) % height
+
+    def placed():
+        names = first_in[:, pl.ds(height, 1), :].reshape(domains, LANES)
+        names = dot(spread, names.astype(BF16))
+        f = iota((iface, iface), 1)
+        for n in range(2):
+            name = jnp.sum(jnp.where(slot == n * height, names, 0.0), axis=1, keepdims=True)
+            place[n * iface : (n + 1) * iface, :] = jnp.where(name == f, 1.0, 0.0).astype(BF16)
 
     def forced(step):
-        all_of(packed.at[step], arrived.at[step], step).wait_recv()
-        got = arrived[step].reshape(iface, LANES).T
+        all_of(step).wait_recv()
+        if step == 0:
+            placed()
+        got = landed[step][:, pl.ds(0, height), :].reshape(iface, LANES).T
         high, low = halves(got)
         both = jnp.concatenate(
             [jnp.concatenate([v[:half], v[half:]], axis=1) for v in (high, low)], axis=0
@@ -296,14 +308,17 @@
     for step in range(ITERS):
         for k in ways:
             part_copy(step, k).wait_send()
-        all_of(packed.at[step], arrived.at[step], step).wait_send()
+        all_of(step).wait_send()
         up[step].wait_send()
         down[step].wait_send()
-    all_of(labels, labels_in, ITERS).wait_send()
 
 def written(final, newer, latest, prior, sem):
+    step = final.shape[0] // CHUNKS
     copies = [
-        pltpu.make_async_copy(src, dst.at[0], sem.at[n])
+        pltpu.make_async_copy(
+            src.at[pl.ds(c * step, step)], dst.at[0, pl.ds(c * step, step)], sem.at[n, c]
+        )
+        for c in range(CHUNKS)
         for n, (src, dst) in enumerate(((final, latest), (newer, prior)))
     ]
     for copy in copies:
@@ -312,6 +327,7 @@
         copy.wait()
 
 
+CHUNKS = 1
 ITERS = 2
 DT2 = 0.5
 KAPPA = 0.5
@@ -329,7 +345,6 @@
     dma = pltpu.SemaphoreType.DMA
     anywhere = pl.BlockSpec(memory_space=pl.ANY)
     vmem = pl.BlockSpec(memory_space=pltpu.VMEM)
-    blocks = (domains, height, LANES)
     scratch = [
         pltpu.VMEM((rows, points), F32),
         pltpu.VMEM((rows, points), F32),
@@ -341,10 +356,10 @@
         pltpu.VMEM((1, iface), F32),
         pltpu.VMEM((ITERS, nsub, rows, iface), F32),
         pltpu.VMEM((ITERS, nsub - 1, rows, iface), F32),
-        pltpu.VMEM((ITERS, *blocks), F32),
-        pltpu.VMEM((ITERS, *blocks), F32),
-        pltpu.VMEM(blocks, F32),
-        pltpu.VMEM(blocks, F32),
+        pltpu.VMEM((domains, height + 1, LANES), F32),
+        pltpu.VMEM((domains, height + 1, LANES), F32),
+        pltpu.VMEM((domains, height, LANES), F32),
+        pltpu.VMEM((domains, height, LANES), F32),
         pltpu.VMEM((2 * edge, 2 * edge), BF16),
         pltpu.VMEM((nsub * rows, 4 * rows), BF16),
         pltpu.VMEM((2 * iface, iface), BF16),
@@ -353,8 +368,8 @@
         dma((8,)),
         dma((ITERS, nsub - 1)),
         dma((ITERS, nsub - 1)),
-        dma((ITERS + 1,)),
-        dma((ITERS + 1,)),
+        dma((ITERS,)),
+        dma((ITERS,)),
         dma((ITERS, 2)),
         dma((ITERS, 2)),
         pltpu.SemaphoreType.REGULAR,
@@ -377,7 +392,7 @@
         out_shape=(out, out),
         in_specs=[anywhere] * 2,
         out_specs=(anywhere, anywhere),
-        scratch_shapes=[dma((2,))],
+        scratch_shapes=[dma((2, CHUNKS))],
         compiler_params=pltpu.CompilerParams(vmem_limit_bytes=1 << 20),
     )(*stepped)
 

time: 44.5 us -> 43.4 us (0.975)
  Pallas kernels: 43.7 us -> 42.7 us
    pallas_call x1, Pallas kernels: 42.4 us -> 41.3 us  [body(): pl.pallas_call(functools.partial(kernel, ny, nz, nsub), out_shape=(pltpu....]
where the time goes in v3:
time: 43.4 us; the launch traced here: 43.3 us
  Pallas kernels  42.7 us (98%)
  between operations  0.64 us (1%)
    pallas_call x1, Pallas kernels, body(): pl.pallas_call(functools.partial(kernel, ny, nz, nsub), out_shape=(pltpu....  41.3 us
    pallas_call x1, Pallas kernels, body(): pl.pallas_call(written, out_shape=(out, out), in_specs=[anywhere] * 2, ou...  1.33 us

profile of v3, /device:TPU:1, one launch (start us, length us, event | category | flops | bytes accessed | tf_op | source)
XLA Modules:
  0.0 43.3 jit_solution(827288204169134101)
XLA Ops:
  0.6 41.3 %shard_map.86 = (f32[64,4096]{1,0:T(8,128)S(1)}, f32[64,4096]{1,0:T(8,128)S(1)}) custom-call(f32[1,64,4096]{2,1,0:T(8,128)} %field.1, f32[1,64,4096]{2,1,0:T(8,128)} %previous.1, f32[1,128,128]{2,1,0:T(8,128)} %stiff.1, f32[1,64,256]{2,1,0:T(8,128)} %bitcast.2, s32[1,256]{1,0:T(1,128)} %bitcast.3, s32[1,256]{1,0:T(1,128)} %face.1, f32[1,256]{1,0:T(1,128)} %weight.1), custom_call_target="tpu_custom_call" | custom-call | tf_op jit(solution)/shard_map/pallas_call | solution.py:377
  42.0 1.3 %shard_map.87 = (f32[1,64,4096]{2,1,0:T(8,128)}, f32[1,64,4096]{2,1,0:T(8,128)}) custom-call(f32[64,4096]{1,0:T(8,128)S(1)} %get-tuple-element.4.final, f32[64,4096]{1,0:T(8,128)S(1)} %get-tuple-element.5.newer), custom_call_target="tpu_custom_call" | custom-call | tf_op jit(solution)/shard_map/pallas_call | solution.py:390

commit v4 on v3

--- a/solution.py
+++ b/solution.py
@@ -34,10 +34,10 @@
 
 def kernel(
     ny, nz, nsub, field, previous, stiff, synth_t, owner, face, weight, final, newer,
-    state, older, halo, stiff_v, synth_v, owner_v, face_v, weight_v,
+    state, older, halo, stiff_v, synth_v, peer_v, owner_v, face_v, weight_v,
     part, part_in, first, first_in, second, second_in,
-    element, operator, pick, place, base,
-    load_sem, part_send, part_recv, pack_send, pack_recv, halo_send, halo_recv, near_sem,
+    element, operator, pick, place, base, ground,
+    load_sem, part_send, part_recv, pack_send, pack_recv, halo_send, halo_recv, synth_send, synth_recv,
 ):
     rows, points = older.shape
     tiles = points // LANES
@@ -59,7 +59,7 @@
         copy.start()
         return copy
 
-    get_synth = load(synth_t.at[0], synth_v, 0)
+    get_synth = load(synth_t.at[0], synth_v.at[sub], 0)
     get_iface = load(field.at[0, :, pl.ds(0, iface)], state.at[:, pl.ds(0, iface)], 1)
     get_owner = load(owner, owner_v, 2)
     get_face = load(face, face_v, 3)
@@ -70,19 +70,25 @@
     )
     get_older = load(previous.at[0], older, 7)
 
+    offsets = [(a, b) for a in range(ny) for b in range(nz)]
+    offsets.sort(key=lambda o: -(min(o[0], ny - o[0]) + min(o[1], nz - o[1])))
+    y_at = [(y + a) % ny * nz for a in range(ny)]
+    z_at = [(z + b) % nz for b in range(nz)]
+    for a, b in offsets:
+        greet(barrier, grp=other, mer=y_at[a] + z_at[b], sub=sub)
     for k in range(1, nsub):
         greet(barrier, grp=grp, mer=mer, sub=(sub + k) % nsub)
-    for k in range(1, nz):
-        greet(barrier, grp=grp, mer=y * nz + (z + k) % nz, sub=sub)
-    for k in range(ny):
-        greet(barrier, grp=other, mer=(y + k) % ny * nz + z, sub=sub)
     greet(barrier, grp=grp, mer=above, sub=sub)
     greet(barrier, grp=grp, mer=below, sub=sub)
 
-    def traces(value, step):
+    def spread_out(value):
         high, low = halves(value)
-        sums = dot(operator[...], jnp.concatenate([high, low, high, low], axis=0))
-        part[step] = sums.reshape(nsub, rows, iface)
+        high, low = high.astype(F32), low.astype(F32)
+        return jnp.concatenate([high, high, low, low], axis=0).T.astype(BF16)
+
+    def doubled(value):
+        high, low = halves(value)
+        return jnp.concatenate([high, low, high, low], axis=0)
 
     def part_copy(step, k):
         to = (sub + k) % nsub
@@ -97,19 +103,6 @@
 
     ways = sorted(range(1, nsub), key=lambda k: -min(k, nsub - k))
 
-    get_synth.wait()
-    high, low = halves(synth_v[...])
-    high, low = high.astype(F32), low.astype(F32)
-    operator[...] = jnp.concatenate([high, high, low, low], axis=0).T.astype(BF16)
-    get_iface.wait()
-    traces(state[:, :iface], 0)
-
-    pl.semaphore_wait(barrier, nsub - 1 + nz - 1 + ny + 2)
-    for k in ways:
-        part_copy(0, k).start()
-    for k in range(ny):
-        greet(near_sem, grp=other, mer=(y + k) % ny * nz + z, sub=sub)
-
     def halo_copy(src, dst, to, step, way):
         return pltpu.make_async_remote_copy(
             src_ref=src,
@@ -131,9 +124,6 @@
         halo_copy(lanes_of(field.at[0], 0), halo.at[0, 1], below, 0, 1),
         halo_copy(lanes_of(newer, 0), halo.at[1, 1], below, 1, 1),
     ]
-    up[0].start()
-    down[0].start()
-
     get_owner.wait()
     get_face.wait()
     get_weight.wait()
@@ -154,10 +144,6 @@
     names = lax.dot_general(chosen, named, NT, preferred_element_type=F32)
     first[:, pl.ds(height, 1), :] = names.reshape(domains, 1, LANES)
 
-    offsets = [(a, b) for a in range(ny) for b in range(nz)]
-    offsets.sort(key=lambda o: -(min(o[0], ny - o[0]) + min(o[1], nz - o[1])))
-    y_at = [(y + a) % ny * nz for a in range(ny)]
-    z_at = [(z + b) % nz for b in range(nz)]
     sent, landed = (first, second), (first_in, second_in)
 
     def send_all(step):
@@ -182,23 +168,23 @@
             device_id_type=MESH,
         )
 
-    def exchange(step):
-        total = part[step, sub]
-        for k in ways[::-1]:
-            part_copy(step, k).wait_recv()
-            total = total + part_in[step, k - 1]
-        total = total * weight_v[...]
-        high, low = halves(total)
+    def exchange(step, total):
+        high, low = halves(total * weight_v[...])
         both = jnp.concatenate([high, low], axis=0)
         out = lax.dot_general(pick[...], both, NT, preferred_element_type=F32)
         out = out + pltpu.roll(out, LANES // 2, 1)
         out = jnp.where(left_half, out[:iface], out[iface:])
         sent[step][:, pl.ds(0, height), :] = out.reshape(domains, height, LANES)
         if step == 0:
-            pl.semaphore_wait(near_sem, ny)
+            pl.semaphore_wait(barrier, domains + nsub - 1 + 2)
         send_all(step)
 
-    exchange(0)
+    def summed(n):
+        total = part[n, sub]
+        for k in ways[::-1]:
+            part_copy(n, k).wait_recv()
+            total = total + part_in[n, k - 1]
+        return total
 
     get_stiff.wait()
     high, low = halves(stiff_v[...] * DT2)
@@ -251,16 +237,48 @@
         if count:
             out[:, lanes_at(n, count)] = stepped(step, n, count)
 
+    get_iface.wait()
     get_state.wait()
     get_older.wait()
+    run(0, newer, itiles, tiles - 1)
+
+    exchange(0, state[:, :iface])
+
+    get_synth.wait()
+
+    def synth_copy(n):
+        to = {"grp": grp, "mer": mer, "sub": (sub + n) % nsub}
+        if n == 0:
+            to = {"grp": other, "mer": mer, "sub": sub}
+        return pltpu.make_async_remote_copy(
+            src_ref=synth_v.at[sub],
+            dst_ref=synth_v.at[sub] if n else peer_v,
+            send_sem=synth_send.at[n],
+            recv_sem=synth_recv.at[n],
+            device_id=to,
+            device_id_type=MESH,
+        )
+
+    for k in [*ways, 0]:
+        synth_copy(k).start()
+    up[0].start()
+    down[0].start()
+
     up[0].wait_recv()
     down[0].wait_recv()
-    base[...] = stepped(0, 0, itiles)
-    run(0, newer, itiles, tiles - 1)
+    ahead = stepped(0, 0, itiles)
+    base[...] = ahead
+    ground[...] = dot(spread_out(synth_v[sub]), doubled(ahead))
     newer[:, pl.ds((tiles - 1) * LANES, LANES)] = stepped(0, tiles - 1, 1)
     up[1].start()
 
-    run(1, final, itiles + 1, tiles - 1)
+    for k in [*ways, 0]:
+        synth_copy(k).wait_recv()
+    high, low = halves(peer_v[...])
+    high_all, low_all = halves(synth_v[...].reshape(nsub * rows, nsub * rows))
+    product = dot(high, high_all) + (dot(high, low_all) + dot(low, high_all))
+    operator[0] = spread_out(product * DT2)
+    operator[1] = spread_out(peer_v[...])
 
     half = LANES // 2
     block = lax.broadcasted_iota(jnp.int32, (iface, domains), 0) // height
@@ -276,7 +294,7 @@
             name = jnp.sum(jnp.where(slot == n * height, names, 0.0), axis=1, keepdims=True)
             place[n * iface : (n + 1) * iface, :] = jnp.where(name == f, 1.0, 0.0).astype(BF16)
 
-    def forced(step):
+    def at_faces(step):
         all_of(step).wait_recv()
         if step == 0:
             placed()
@@ -286,31 +304,36 @@
             [jnp.concatenate([v[:half], v[half:]], axis=1) for v in (high, low)], axis=0
         )
         out = dot(both, place[...])
-        return base[...] + DT2 * (out[:rows] + out[rows:])
-
-    mid = forced(0)
-    newer[:, pl.ds(0, iface)] = mid
-    traces(mid, 1)
+        return out[:rows] + out[rows:]
+
+    sums = doubled(at_faces(0))
+    part[0] = (ground[...] + dot(operator[0], sums)).reshape(nsub, rows, iface)
+    for k in ways:
+        part_copy(0, k).start()
+    part[1] = dot(operator[1], sums).reshape(nsub, rows, iface)
+    exchange(1, summed(0))
+
     for k in ways:
         part_copy(1, k).start()
+    run(1, final, itiles + 1, tiles - 1)
+    newer[:, pl.ds(0, iface)] = base[...] + DT2 * summed(1)
     down[1].start()
-
     up[1].wait_recv()
     ahead = stepped(1, 0, itiles + 1)
     base[...] = ahead[:, :iface]
     final[:, pl.ds(iface, LANES)] = ahead[:, iface:]
-
-    exchange(1)
     down[1].wait_recv()
     final[:, pl.ds((tiles - 1) * LANES, LANES)] = stepped(1, tiles - 1, 1)
 
-    final[:, pl.ds(0, iface)] = forced(1)
+    final[:, pl.ds(0, iface)] = base[...] + DT2 * at_faces(1)
     for step in range(ITERS):
         for k in ways:
             part_copy(step, k).wait_send()
         all_of(step).wait_send()
         up[step].wait_send()
         down[step].wait_send()
+    for k in range(nsub):
+        synth_copy(k).wait_send()
 
 def written(final, newer, latest, prior, sem):
     step = final.shape[0] // CHUNKS
@@ -350,6 +373,7 @@
         pltpu.VMEM((rows, points), F32),
         pltpu.VMEM((ITERS, 2, rows, LANES), F32),
         pltpu.VMEM((edge, edge), F32),
+        pltpu.VMEM((nsub, rows, nsub * rows), F32),
         pltpu.VMEM((rows, nsub * rows), F32),
         pltpu.VMEM((1, iface), jnp.int32),
         pltpu.VMEM((1, iface), jnp.int32),
@@ -361,10 +385,11 @@
         pltpu.VMEM((domains, height, LANES), F32),
         pltpu.VMEM((domains, height, LANES), F32),
         pltpu.VMEM((2 * edge, 2 * edge), BF16),
-        pltpu.VMEM((nsub * rows, 4 * rows), BF16),
+        pltpu.VMEM((2, nsub * rows, 4 * rows), BF16),
         pltpu.VMEM((2 * iface, iface), BF16),
         pltpu.VMEM((2 * iface, iface), BF16),
         pltpu.VMEM((rows, iface), F32),
+        pltpu.VMEM((nsub * rows, iface), F32),
         dma((8,)),
         dma((ITERS, nsub - 1)),
         dma((ITERS, nsub - 1)),
@@ -372,7 +397,8 @@
         dma((ITERS,)),
         dma((ITERS, 2)),
         dma((ITERS, 2)),
-        pltpu.SemaphoreType.REGULAR,
+        dma((nsub,)),
+        dma((nsub,)),
     ]
     stepped = pl.pallas_call(
         functools.partial(kernel, ny, nz, nsub),

time: 43.4 us -> 41.6 us (0.959)
  Pallas kernels: 42.7 us -> 40.8 us
    pallas_call x1, Pallas kernels: 41.3 us -> 39.5 us  [body(): pl.pallas_call(functools.partial(kernel, ny, nz, nsub), out_shape=(pltpu....]
where the time goes in v4:
time: 41.6 us; the launch traced here: 41.4 us
  Pallas kernels  40.8 us (98%)
  between operations  0.64 us (2%)
    pallas_call x1, Pallas kernels, body(): pl.pallas_call(functools.partial(kernel, ny, nz, nsub), out_shape=(pltpu....  39.5 us
    pallas_call x1, Pallas kernels, body(): pl.pallas_call(written, out_shape=(out, out), in_specs=[anywhere] * 2, ou...  1.33 us

profile of v4, /device:TPU:1, one launch (start us, length us, event | category | flops | bytes accessed | tf_op | source)
XLA Modules:
  0.0 41.4 jit_solution(10335351892075952871)
XLA Ops:
  0.6 39.5 %shard_map.86 = (f32[64,4096]{1,0:T(8,128)S(1)}, f32[64,4096]{1,0:T(8,128)S(1)}) custom-call(f32[1,64,4096]{2,1,0:T(8,128)} %field.1, f32[1,64,4096]{2,1,0:T(8,128)} %previous.1, f32[1,128,128]{2,1,0:T(8,128)} %stiff.1, f32[1,64,256]{2,1,0:T(8,128)} %bitcast.2, s32[1,256]{1,0:T(1,128)} %bitcast.3, s32[1,256]{1,0:T(1,128)} %face.1, f32[1,256]{1,0:T(1,128)} %weight.1), custom_call_target="tpu_custom_call" | custom-call | tf_op jit(solution)/shard_map/pallas_call | solution.py:403
  40.1 1.3 %shard_map.87 = (f32[1,64,4096]{2,1,0:T(8,128)}, f32[1,64,4096]{2,1,0:T(8,128)}) custom-call(f32[64,4096]{1,0:T(8,128)S(1)} %get-tuple-element.4.final, f32[64,4096]{1,0:T(8,128)S(1)} %get-tuple-element.5.newer), custom_call_target="tpu_custom_call" | custom-call | tf_op jit(solution)/shard_map/pallas_call | solution.py:416

commit v5 on v4

--- a/solution.py
+++ b/solution.py
@@ -36,7 +36,7 @@
     ny, nz, nsub, field, previous, stiff, synth_t, owner, face, weight, final, newer,
     state, older, halo, stiff_v, synth_v, peer_v, owner_v, face_v, weight_v,
     part, part_in, first, first_in, second, second_in,
-    element, operator, pick, place, base, ground,
+    element, operator, pick, place, base, ground, sums,
     load_sem, part_send, part_recv, pack_send, pack_recv, halo_send, halo_recv, synth_send, synth_recv,
 ):
     rows, points = older.shape
@@ -46,13 +46,24 @@
     itiles = iface // LANES
     grp, mer, sub = lax.axis_index("grp"), lax.axis_index("mer"), lax.axis_index("sub")
     other = 1 - grp
-    y, z = mer // nz, mer % nz
-    above, below = (mer + 1) % domains, (mer + domains - 1) % domains
+    y, z = lax.div(mer, nz), lax.rem(mer, nz)
+    above, below = lax.rem(mer + 1, domains), lax.rem(mer + domains - 1, domains)
 
     barrier = pltpu.get_barrier_semaphore()
 
     def greet(sem, **where):
         pl.semaphore_signal(sem, inc=1, device_id=where, device_id_type=MESH)
+
+    offsets = [(a, b) for a in range(ny) for b in range(nz)]
+    offsets.sort(key=lambda o: -(min(o[0], ny - o[0]) + min(o[1], nz - o[1])))
+    y_at = [lax.rem(y + a, ny) * nz for a in range(ny)]
+    z_at = [lax.rem(z + b, nz) for b in range(nz)]
+    for a, b in offsets:
+        greet(barrier, grp=other, mer=y_at[a] + z_at[b], sub=sub)
+    for k in range(1, nsub):
+        greet(barrier, grp=grp, mer=mer, sub=lax.rem(sub + k, nsub))
+    greet(barrier, grp=grp, mer=above, sub=sub)
+    greet(barrier, grp=grp, mer=below, sub=sub)
 
     def load(src, dst, n):
         copy = pltpu.make_async_copy(src, dst, load_sem.at[n])
@@ -70,17 +81,6 @@
     )
     get_older = load(previous.at[0], older, 7)
 
-    offsets = [(a, b) for a in range(ny) for b in range(nz)]
-    offsets.sort(key=lambda o: -(min(o[0], ny - o[0]) + min(o[1], nz - o[1])))
-    y_at = [(y + a) % ny * nz for a in range(ny)]
-    z_at = [(z + b) % nz for b in range(nz)]
-    for a, b in offsets:
-        greet(barrier, grp=other, mer=y_at[a] + z_at[b], sub=sub)
-    for k in range(1, nsub):
-        greet(barrier, grp=grp, mer=mer, sub=(sub + k) % nsub)
-    greet(barrier, grp=grp, mer=above, sub=sub)
-    greet(barrier, grp=grp, mer=below, sub=sub)
-
     def spread_out(value):
         high, low = halves(value)
         high, low = high.astype(F32), low.astype(F32)
@@ -91,7 +91,7 @@
         return jnp.concatenate([high, low, high, low], axis=0)
 
     def part_copy(step, k):
-        to = (sub + k) % nsub
+        to = lax.rem(sub + k, nsub)
         return pltpu.make_async_remote_copy(
             src_ref=part.at[step, to],
             dst_ref=part_in.at[step, k - 1],
@@ -247,7 +247,7 @@
     get_synth.wait()
 
     def synth_copy(n):
-        to = {"grp": grp, "mer": mer, "sub": (sub + n) % nsub}
+        to = {"grp": grp, "mer": mer, "sub": lax.rem(sub + n, nsub)}
         if n == 0:
             to = {"grp": other, "mer": mer, "sub": sub}
         return pltpu.make_async_remote_copy(
@@ -289,10 +289,12 @@
     def placed():
         names = first_in[:, pl.ds(height, 1), :].reshape(domains, LANES)
         names = dot(spread, names.astype(BF16))
-        f = iota((iface, iface), 1)
+        f = iota((iface, iface), 1).astype(BF16)
+        one, zero = jnp.ones((iface, iface), BF16), jnp.zeros((iface, iface), BF16)
         for n in range(2):
             name = jnp.sum(jnp.where(slot == n * height, names, 0.0), axis=1, keepdims=True)
-            place[n * iface : (n + 1) * iface, :] = jnp.where(name == f, 1.0, 0.0).astype(BF16)
+            name = jnp.broadcast_to(name, (iface, iface)).astype(BF16)
+            place[n * iface : (n + 1) * iface, :] = jnp.where(name == f, one, zero)
 
     def at_faces(step):
         all_of(step).wait_recv()
@@ -306,13 +308,13 @@
         out = dot(both, place[...])
         return out[:rows] + out[rows:]
 
-    sums = doubled(at_faces(0))
-    part[0] = (ground[...] + dot(operator[0], sums)).reshape(nsub, rows, iface)
+    sums[...] = doubled(at_faces(0))
+    part[0] = (ground[...] + dot(operator[0], sums[...])).reshape(nsub, rows, iface)
     for k in ways:
         part_copy(0, k).start()
-    part[1] = dot(operator[1], sums).reshape(nsub, rows, iface)
     exchange(1, summed(0))
 
+    part[1] = dot(operator[1], sums[...]).reshape(nsub, rows, iface)
     for k in ways:
         part_copy(1, k).start()
     run(1, final, itiles + 1, tiles - 1)
@@ -325,7 +327,6 @@
     down[1].wait_recv()
     final[:, pl.ds((tiles - 1) * LANES, LANES)] = stepped(1, tiles - 1, 1)
 
-    final[:, pl.ds(0, iface)] = base[...] + DT2 * at_faces(1)
     for step in range(ITERS):
         for k in ways:
             part_copy(step, k).wait_send()
@@ -334,6 +335,8 @@
         down[step].wait_send()
     for k in range(nsub):
         synth_copy(k).wait_send()
+    final[:, pl.ds(0, iface)] = base[...] + DT2 * at_faces(1)
+
 
 def written(final, newer, latest, prior, sem):
     step = final.shape[0] // CHUNKS
@@ -390,6 +393,7 @@
         pltpu.VMEM((2 * iface, iface), BF16),
         pltpu.VMEM((rows, iface), F32),
         pltpu.VMEM((nsub * rows, iface), F32),
+        pltpu.VMEM((4 * rows, iface), BF16),
         dma((8,)),
         dma((ITERS, nsub - 1)),
         dma((ITERS, nsub - 1)),

time: 41.6 us -> 41.5 us (level)
  no operation moved by 1% of the time
where the time goes in v5:
time: 41.5 us; the launch traced here: 41.3 us
  Pallas kernels  40.7 us (98%)
  between operations  0.64 us (2%)
    pallas_call x1, Pallas kernels, body(): pl.pallas_call(functools.partial(kernel, ny, nz, nsub), out_shape=(pltpu....  39.3 us
    pallas_call x1, Pallas kernels, body(): pl.pallas_call(written, out_shape=(out, out), in_specs=[anywhere] * 2, ou...  1.33 us

profile of v5, /device:TPU:1, one launch (start us, length us, event | category | flops | bytes accessed | tf_op | source)
XLA Modules:
  0.0 41.3 jit_solution(17827208187371296099)
XLA Ops:
  0.6 39.3 %shard_map.86 = (f32[64,4096]{1,0:T(8,128)S(1)}, f32[64,4096]{1,0:T(8,128)S(1)}) custom-call(f32[1,64,4096]{2,1,0:T(8,128)} %field.1, f32[1,64,4096]{2,1,0:T(8,128)} %previous.1, f32[1,128,128]{2,1,0:T(8,128)} %stiff.1, f32[1,64,256]{2,1,0:T(8,128)} %bitcast.2, s32[1,256]{1,0:T(1,128)} %bitcast.3, s32[1,256]{1,0:T(1,128)} %face.1, f32[1,256]{1,0:T(1,128)} %weight.1), custom_call_target="tpu_custom_call" | custom-call | tf_op jit(solution)/shard_map/pallas_call | solution.py:407
  40.0 1.3 %shard_map.87 = (f32[1,64,4096]{2,1,0:T(8,128)}, f32[1,64,4096]{2,1,0:T(8,128)}) custom-call(f32[64,4096]{1,0:T(8,128)S(1)} %get-tuple-element.4.final, f32[64,4096]{1,0:T(8,128)S(1)} %get-tuple-element.5.newer), custom_call_target="tpu_custom_call" | custom-call | tf_op jit(solution)/shard_map/pallas_call | solution.py:420

commit v6 on v5

--- a/solution.py
+++ b/solution.py
@@ -135,9 +135,8 @@
     late = (rank >= height).astype(F32)
     row = own * height + rank - height * late
     hit = jnp.where(i == row, 1.0, 0.0)
-    pick[0:iface, :] = (hit * (1.0 - late)).astype(BF16)
-    pick[iface:, :] = (hit * late).astype(BF16)
-    left_half = lax.broadcasted_iota(jnp.int32, (iface, LANES), 1) < LANES // 2
+    picked = jnp.concatenate([(hit * (1.0 - late)).astype(BF16), (hit * late).astype(BF16)], axis=1)
+    pick[...] = jnp.concatenate([picked, picked], axis=1)
 
     named = jnp.where(iota((LANES, iface), 0) == rank, face_v[...].astype(F32), 0.0).astype(BF16)
     chosen = jnp.where(iota((domains, iface), 0) == own, 1.0, 0.0).astype(BF16)
@@ -170,10 +169,15 @@
 
     def exchange(step, total):
         high, low = halves(total * weight_v[...])
-        both = jnp.concatenate([high, low], axis=0)
+        none = jnp.zeros_like(high)
+        both = jnp.concatenate(
+            [
+                jnp.concatenate([high, none, low, none], axis=1),
+                jnp.concatenate([none, high, none, low], axis=1),
+            ],
+            axis=0,
+        )
         out = lax.dot_general(pick[...], both, NT, preferred_element_type=F32)
-        out = out + pltpu.roll(out, LANES // 2, 1)
-        out = jnp.where(left_half, out[:iface], out[iface:])
         sent[step][:, pl.ds(0, height), :] = out.reshape(domains, height, LANES)
         if step == 0:
             pl.semaphore_wait(barrier, domains + nsub - 1 + 2)
@@ -389,7 +393,7 @@
         pltpu.VMEM((domains, height, LANES), F32),
         pltpu.VMEM((2 * edge, 2 * edge), BF16),
         pltpu.VMEM((2, nsub * rows, 4 * rows), BF16),
-        pltpu.VMEM((2 * iface, iface), BF16),
+        pltpu.VMEM((iface, 4 * iface), BF16),
         pltpu.VMEM((2 * iface, iface), BF16),
         pltpu.VMEM((rows, iface), F32),
         pltpu.VMEM((nsub * rows, iface), F32),

time: 41.5 us -> 41.5 us (level)
  no operation moved by 1% of the time
where the time goes in v6:
time: 41.5 us; the launch traced here: 41.3 us
  Pallas kernels  40.7 us (98%)
  between operations  0.64 us (2%)
    pallas_call x1, Pallas kernels, body(): pl.pallas_call(functools.partial(kernel, ny, nz, nsub), out_shape=(pltpu....  39.4 us
    pallas_call x1, Pallas kernels, body(): pl.pallas_call(written, out_shape=(out, out), in_specs=[anywhere] * 2, ou...  1.33 us

profile of v6, /device:TPU:1, one launch (start us, length us, event | category | flops | bytes accessed | tf_op | source)
XLA Modules:
  0.0 41.3 jit_solution(13159567590419860811)
XLA Ops:
  0.6 39.4 %shard_map.86 = (f32[64,4096]{1,0:T(8,128)S(1)}, f32[64,4096]{1,0:T(8,128)S(1)}) custom-call(f32[1,64,4096]{2,1,0:T(8,128)} %field.1, f32[1,64,4096]{2,1,0:T(8,128)} %previous.1, f32[1,128,128]{2,1,0:T(8,128)} %stiff.1, f32[1,64,256]{2,1,0:T(8,128)} %bitcast.2, s32[1,256]{1,0:T(1,128)} %bitcast.3, s32[1,256]{1,0:T(1,128)} %face.1, f32[1,256]{1,0:T(1,128)} %weight.1), custom_call_target="tpu_custom_call" | custom-call | tf_op jit(solution)/shard_map/pallas_call | solution.py:411
  40.0 1.3 %shard_map.87 = (f32[1,64,4096]{2,1,0:T(8,128)}, f32[1,64,4096]{2,1,0:T(8,128)}) custom-call(f32[64,4096]{1,0:T(8,128)S(1)} %get-tuple-element.4.final, f32[64,4096]{1,0:T(8,128)S(1)} %get-tuple-element.5.newer), custom_call_target="tpu_custom_call" | custom-call | tf_op jit(solution)/shard_map/pallas_call | solution.py:424
